TPU v7x, 256 devices: a whole 4x4x8 slice. The times are simulated.
256 devices in a mesh: blk: 32 (over z_lo, x, core), grp: 8 (over z_hi, y).
Axes of the slice: x: 4, y: 4, z: 8 (z_hi: 2, z_lo: 4; z = z_hi * 4 + z_lo), core: 2. Of those that a mesh axis runs over, the one named last changes fastest.
Arguments:
- lambda_init: float32 [131072, 256], P('blk'), may hold values from 0.1 to 200
- gamma_init: float32 [32768, 256], P(('blk', 'grp')), may hold values from 0.5 to 20
- dmr_table: float32 [1024, 256], replicated, may hold values from -3 to 3
- features: int32 [32768, 4], P(('blk', 'grp')), may hold values from 0 to 1023
- counts: int32 [256, 4, 6, 128, 128], P(('blk', 'grp')), may hold values from 0 to 3
- tile_cols: int32 [256, 4, 6], P(('blk', 'grp')), may hold values from 0 to 31, as said below
- live_slots: int32 [256, 4], P(('blk', 'grp')), may hold values from 1 to 6, as said below
Outputs:
- gamma_out: float32 [32768, 256], P(('blk', 'grp'))
- lambda_out: float32 [131072, 256], P(('blk', 'grp'))
Inputs may be any that keep to these rules, and one draw needn't show every extreme that they name: `tile_cols`: within one row tile and substep the 6 column tiles are distinct. Slots 0 to live_slots - 1 of a row tile and substep are in use, the others are padding; row tile 0 uses all 6 slots in substep 0.
All inputs are finite; a program needn't handle non-finite values.
Results may differ from a plain program's by a relative error of at most 0.009.
Values sent between devices are 32-bit elements; how exact they have to be, the bound alone decides.
A program may use at most 128 MiB of HBM per device.

v0:
```python
import jax
import jax.numpy as jnp
from jax import lax
from jax.sharding import PartitionSpec as P

STRATA = 4
LOCAL = 3


pass_bits = (0, 1, 0)
step_weight = 0.5
word_prior = 0.05


def partner(value, axis, bit):
    mask = 2**bit
    pairs = [(source, source ^ mask) for source in range(lax.axis_size(axis))]
    return lax.ppermute(value, axis, pairs)


def expected_theta(doc_gamma):
    return jnp.exp(
        lax.digamma(doc_gamma) - lax.digamma(jnp.sum(doc_gamma, axis=1, keepdims=True))
    ).astype(jnp.bfloat16)


def update_padded(doc_gamma, doc_alpha, beta_exp, tile_counts, column_ids, live_count):
    rows, slots = column_ids.shape
    tile = tile_counts.shape[-1]
    topics = beta_exp.shape[1]
    columns = beta_exp.shape[0] // tile
    word_tiles = beta_exp.reshape(columns, tile, topics)[column_ids]
    active = jnp.arange(slots)[None, :] < live_count[:, None]
    tile_weight = jnp.where(active[:, :, None, None], tile_counts, 0).astype(jnp.float32)

    def ratio_of(theta_exp):
        theta_rows = theta_exp.reshape(rows, tile, topics)
        denom_tiles = jnp.einsum(
            "rdk,rswk->rsdw", theta_rows, word_tiles, preferred_element_type=jnp.float32
        )
        return (theta_rows, (tile_weight / denom_tiles).astype(jnp.bfloat16))

    for repeat in range(LOCAL):
        theta_exp = expected_theta(doc_gamma)
        theta_rows, count_ratio = ratio_of(theta_exp)
        contrib = jnp.einsum(
            "rsdw,rswk->rdk", count_ratio, word_tiles, preferred_element_type=jnp.float32
        )
        doc_gamma = doc_alpha + theta_exp.astype(jnp.float32) * contrib.reshape(doc_gamma.shape)
    theta_exp = expected_theta(doc_gamma)
    theta_rows, count_ratio = ratio_of(theta_exp)
    stat_tiles = jnp.einsum(
        "rsdw,rdk->rswk", count_ratio, theta_rows, preferred_element_type=jnp.float32
    )
    selector = (column_ids.reshape(-1)[None, :] == jnp.arange(columns)[:, None]).astype(jnp.float32)
    accumulated = jnp.dot(
        selector,
        stat_tiles.reshape(rows * slots, tile * topics),
        precision=lax.Precision.HIGHEST,
        preferred_element_type=jnp.float32,
    )
    partial_value = (beta_exp.astype(jnp.float32) * accumulated.reshape(beta_exp.shape)).astype(
        jnp.bfloat16
    )
    return (doc_gamma, partial_value)


def on_device(lambda_init, gamma_init, dmr_table, features, counts, tile_cols, live_slots):
    groups = lax.axis_size("grp")
    doc_alpha = jnp.exp(jnp.sum(jnp.take(dmr_table, features, axis=0), axis=1))
    topic_panel = lambda_init
    doc_gamma = gamma_init
    ahead = [(counts[:, step], tile_cols[:, step], live_slots[:, step]) for step in range(STRATA)]
    for substep in range(STRATA):
        topic_totals = lax.psum(jnp.sum(topic_panel, axis=0), "blk")
        beta_exp = jnp.exp(lax.digamma(topic_panel) - lax.digamma(topic_totals)[None, :]).astype(
            jnp.bfloat16
        )
        tile_counts, column_ids, live_count = ahead[substep]
        doc_gamma, partial_value = update_padded(
            doc_gamma, doc_alpha, beta_exp, tile_counts, column_ids, live_count
        )
        partial_wide = partial_value.astype(jnp.float32)
        topic_panel = (1.0 - step_weight) * topic_panel + step_weight * (
            word_prior + groups * partial_wide
        )
        if substep + 1 < STRATA:
            topic_panel = partner(topic_panel, "blk", pass_bits[substep])
    returned = partner(topic_panel, "blk", 1)
    lambda_out = lax.psum_scatter(returned, "grp", scatter_dimension=0, tiled=True) / groups
    return (doc_gamma, lambda_out)


def solution(mesh):
    placed = (
        P("blk", None),
        P(("blk", "grp"), None),
        P(),
        P(("blk", "grp"), None),
        P(("blk", "grp"), None, None, None, None),
        P(("blk", "grp"), None, None),
        P(("blk", "grp"), None),
    )
    return jax.shard_map(
        on_device,
        mesh=mesh,
        in_specs=placed,
        out_specs=(P(("blk", "grp"), None), P(("blk", "grp"), None)),
        check_vma=False,
    )
```

profile of v0, /device:TPU:1, one launch (start us, length us, event | category | flops | bytes accessed | tf_op | source)
XLA Modules:
  0.0 971.0 jit_solution(11349944712622576817)
XLA Ops:
  14.2 2.7 reduce_sum.176
  17.0 70.1 %psum.28 = f32[256]{0:T(256)S(1)} all-reduce(f32[256]{0:T(256)S(1)} %reduce_sum.176), channel_id=1, replica_groups=mesh['blk'=32,'grp'=8] {'blk'}, use_global_device_ids=true, to_apply=%region_3.4 | all-reduce | flops 256 | bytes 2048 | tf_op jit(solution)/shard_map/psum | solution.py:75
  87.2 31.2 %fusion.4 = bf16[4096,256]{1,0:T(8,128)(2,1)} fusion(f32[4096,256]{1,0:T(8,128)} %param.7, f32[256]{0:T(256)S(1)} %compare_select_fusion.20), kind=kLoop, calls=%fused_computation.17 | loop fusion | flops 80740352 | bytes 6292480 | tf_op jit(solution)/shard_map/convert_element_type | solution.py:76
  126.1 2.3 fusion.1346
  133.5 3.7 fusion.796
  137.2 4.9 reshape.2574
  142.1 33.2 %add_multiply_fusion.3 = f32[4096,256]{1,0:T(8,128)} fusion(f32[4096,256]{1,0:T(8,128)} %param.7, f32[4096,256]{1,0:T(8,128)} %reshape.2574, f32[256]{0:T(256)S(1)} %copy-done.7), kind=kLoop, calls=%fused_computation.39 | loop fusion | flops 89128960 | bytes 12583936 | tf_op jit(solution)/shard_map/add | solution.py:84
  175.4 5.2 collective-permute-start
  181.4 6.3 collective-permute-done
  187.7 2.7 reduce_sum.180
  190.5 67.5 %psum.29 = f32[256]{0:T(256)S(1)} all-reduce(f32[256]{0:T(256)S(1)} %reduce_sum.180), channel_id=1, replica_groups=mesh['blk'=32,'grp'=8] {'blk'}, use_global_device_ids=true, to_apply=%region_8.9 | all-reduce | flops 256 | bytes 2048 | tf_op jit(solution)/shard_map/psum | solution.py:75
  258.0 31.1 %fusion.9 = bf16[4096,256]{1,0:T(8,128)(2,1)} fusion(f32[4096,256]{1,0:T(8,128)} %collective-permute-done, f32[256]{0:T(256)S(1)} %compare_select_fusion.16), kind=kLoop, calls=%fused_computation.22 | loop fusion | flops 80740352 | bytes 6292480 | tf_op jit(solution)/shard_map/convert_element_type | solution.py:76
  299.3 3.7 fusion.797
  303.0 4.9 reshape.2582
  307.9 33.2 %add_multiply_fusion.2 = f32[4096,256]{1,0:T(8,128)} fusion(f32[4096,256]{1,0:T(8,128)} %collective-permute-done, f32[4096,256]{1,0:T(8,128)} %reshape.2582, f32[256]{0:T(256)S(1)} %compare_select_fusion.16), kind=kLoop, calls=%fused_computation.37 | loop fusion | flops 89128960 | bytes 12583936 | tf_op jit(solution)/shard_map/add | solution.py:84
  342.2 90.8 %collective-permute-done.1 = f32[4096,256]{1,0:T(8,128)} collective-permute-done((f32[4096,256]{1,0:T(8,128)}, f32[4096,256]{1,0:T(8,128)}, u32[]{:S(2)}, u32[]{:S(2)}) %collective-permute-start.1) | collective-permute-done | bytes 4194336 | tf_op jit(solution)/shard_map/ppermute | solution.py:18
  433.0 2.7 reduce_sum.184
  435.7 68.4 %psum.30 = f32[256]{0:T(256)S(1)} all-reduce(f32[256]{0:T(256)S(1)} %reduce_sum.184), channel_id=1, replica_groups=mesh['blk'=32,'grp'=8] {'blk'}, use_global_device_ids=true, to_apply=%region_13.14 | all-reduce | flops 256 | bytes 2048 | tf_op jit(solution)/shard_map/psum | solution.py:75
  504.2 31.1 %fusion.14 = bf16[4096,256]{1,0:T(8,128)(2,1)} fusion(f32[4096,256]{1,0:T(8,128)} %collective-permute-done.1, f32[256]{0:T(256)S(1)} %compare_select_fusion.12), kind=kLoop, calls=%fused_computation.27 | loop fusion | flops 80740352 | bytes 6292480 | tf_op jit(solution)/shard_map/convert_element_type | solution.py:76
  538.1 2.3 fusion.1364
  544.8 3.7 fusion.798
  548.6 4.9 reshape.2590
  553.4 33.2 %add_multiply_fusion.1 = f32[4096,256]{1,0:T(8,128)} fusion(f32[4096,256]{1,0:T(8,128)} %collective-permute-done.1, f32[4096,256]{1,0:T(8,128)} %reshape.2590, f32[256]{0:T(256)S(1)} %compare_select_fusion.12), kind=kLoop, calls=%fused_computation.35 | loop fusion | flops 89128960 | bytes 12583936 | tf_op jit(solution)/shard_map/add | solution.py:84
  588.4 6.3 collective-permute-done.2
  594.7 2.7 reduce_sum.188
  597.4 67.1 %psum.31 = f32[256]{0:T(256)S(1)} all-reduce(f32[256]{0:T(256)S(1)} %reduce_sum.188), channel_id=1, replica_groups=mesh['blk'=32,'grp'=8] {'blk'}, use_global_device_ids=true, to_apply=%region_18.19 | all-reduce | flops 256 | bytes 2048 | tf_op jit(solution)/shard_map/psum | solution.py:75
  664.6 31.0 %fusion.19 = bf16[4096,256]{1,0:T(8,128)(2,1)} fusion(f32[4096,256]{1,0:T(8,128)} %collective-permute-done.2, f32[256]{0:T(256)S(1)} %compare_select_fusion.8), kind=kLoop, calls=%fused_computation.32 | loop fusion | flops 80740352 | bytes 6292480 | tf_op jit(solution)/shard_map/convert_element_type | solution.py:76
  706.0 3.7 fusion.799
  709.7 4.9 reshape.2598
  714.7 31.3 %add_multiply_fusion = f32[4096,256]{1,0:T(8,128)S(1)} fusion(f32[4096,256]{1,0:T(8,128)} %collective-permute-done.2, f32[4096,256]{1,0:T(8,128)} %reshape.2598, f32[256]{0:T(256)S(1)} %compare_select_fusion.8), kind=kLoop, calls=%fused_computation.33 | loop fusion | flops 89128960 | bytes 12583936 | tf_op jit(solution)/shard_map/add | solution.py:84
  746.1 91.4 %collective-permute-done.3 = f32[4096,256]{1,0:T(8,128)} collective-permute-done((f32[4096,256]{1,0:T(8,128)S(1)}, f32[4096,256]{1,0:T(8,128)}, u32[]{:S(2)}, u32[]{:S(2)}) %collective-permute-start.3) | collective-permute-done | bytes 4194336 | tf_op jit(solution)/shard_map/ppermute | solution.py:18
  837.5 124.5 %reduce-scatter.2.cloned.1.call-done = f32[512,256]{1,0:T(8,128)} async-done(((f32[4096,256]{1,0:T(8,128)}), f32[512,256]{1,0:T(8,128)}) %reduce-scatter.2.cloned.1.call-update) | async-done | bytes 524304 | tf_op jit(solution)/shard_map/reduce_scatter | solution.py:90
  (114 shorter events, 53.1 us)
Async XLA Ops:
  7.2 4.6 copy-start
  7.2 954.9 %reduce-scatter.2.cloned.1.call-start = ((), (), s32[]{:S(2)}) async-start(), calls=%async_computation.1 | async-start | bytes 4718592 | tf_op jit(solution)/shard_map/reduce_scatter | solution.py:90
  17.0 101.4 %copy-start.2 = (s32[1,4,6,128,128]{4,3,2,1,0:T(8,128)S(1)}, s32[1,4,6,128,128]{4,3,2,1,0:T(8,128)}, u32[]{:S(2)}) copy-start(s32[1,4,6,128,128]{4,3,2,1,0:T(8,128)} %param.11) | copy-start | bytes 4718596
  87.1 32.1 %copy-start.6 = (f32[256]{0:T(256)}, f32[256]{0:T(256)S(1)}, u32[]{:S(2)}) copy-start(f32[256]{0:T(256)S(1)} %compare_select_fusion.20) | copy-start | bytes 3076
  87.1 32.3 %copy-start.5 = (s32[1,4]{1,0:T(1,128)S(1)}, s32[1,4]{1,0:T(1,128)}, u32[]{:S(2)}) copy-start(s32[1,4]{1,0:T(1,128)} %param.13) | copy-start | bytes 52
  87.2 33.7 %copy-start.4 = (f32[128,256]{1,0:T(8,128)S(1)}, f32[128,256]{1,0:T(8,128)}, u32[]{:S(2)}) copy-start(f32[128,256]{1,0:T(8,128)} %param.8) | copy-start | bytes 393220
  128.5 5.0 copy-start.14
  131.9 0.6 copy-start.18
  137.2 4.9 copy-start.7
  142.1 38.5 %copy-start.3 = (s32[1,1,6,128,128]{4,3,2,1,0:T(8,128)S(1)}, s32[1,1,6,128,128]{4,3,2,1,0:T(8,128)}, u32[]{:S(2)}) copy-start(s32[1,1,6,128,128]{4,3,2,1,0:T(8,128)} %get-tuple-element.4) | copy-start | bytes 1179652
  142.1 39.3 %copy-start.10 = (s32[6]{0:T(128)S(1)}, s32[6]{0:T(128)}, u32[]{:S(2)}) copy-start(s32[6]{0:T(128)} %get-tuple-element.11) | copy-start | bytes 76
  175.4 12.4 %collective-permute-start = (f32[4096,256]{1,0:T(8,128)}, f32[4096,256]{1,0:T(8,128)}, u32[]{:S(2)}, u32[]{:S(2)}) collective-permute-start(f32[4096,256]{1,0:T(8,128)} %add_multiply_fusion.3), channel_id=1, source_target_pairs={{0,8},{8,0},{16,24},{24,16},{32,40},{40,32},{48,56},{56,48},{64,72... | collective-permute-start | bytes 12582920 | tf_op jit(solution)/shard_map/ppermute | solution.py:18
  258.0 33.2 %copy-start.19 = (bf16[128,256]{1,0:T(8,128)(2,1)S(1)}, bf16[128,256]{1,0:T(8,128)(2,1)}, u32[]{:S(2)}) copy-start(bf16[128,256]{1,0:T(8,128)(2,1)} %copy-done.18) | copy-start | bytes 196612
  294.3 5.0 copy-start.13
  297.7 0.6 copy-start.16
  307.9 34.3 %copy-start.9 = (s32[6]{0:T(128)S(1)}, s32[6]{0:T(128)}, u32[]{:S(2)}) copy-start(s32[6]{0:T(128)} %get-tuple-element.13) | copy-start | bytes 76
  341.1 91.9 %collective-permute-start.1 = (f32[4096,256]{1,0:T(8,128)}, f32[4096,256]{1,0:T(8,128)}, u32[]{:S(2)}, u32[]{:S(2)}) collective-permute-start(f32[4096,256]{1,0:T(8,128)} %add_multiply_fusion.2), channel_id=1, source_target_pairs={{0,16},{8,24},{16,0},{24,8},{32,48},{40,56},{48,32},{56,40},{64,80... | collective-permute-start | bytes 12582920 | tf_op jit(solution)/shard_map/ppermute | solution.py:18
  504.2 33.2 %copy-start.17 = (bf16[128,256]{1,0:T(8,128)(2,1)S(1)}, bf16[128,256]{1,0:T(8,128)(2,1)}, u32[]{:S(2)}) copy-start(bf16[128,256]{1,0:T(8,128)(2,1)} %copy-done.16) | copy-start | bytes 196612
  540.5 4.3 copy-start.12
  553.4 34.9 %copy-start.8 = (s32[6]{0:T(128)S(1)}, s32[6]{0:T(128)}, u32[]{:S(2)}) copy-start(s32[6]{0:T(128)} %get-tuple-element.10) | copy-start | bytes 76
  586.6 8.1 collective-permute-start.2
  703.2 2.3 copy-start.15
  703.3 2.7 copy-start.11
  714.7 249.2 %copy-start.1 = (f32[1024,256]{1,0:T(8,128)S(1)}, f32[1024,256]{1,0:T(8,128)}, u32[]{:S(2)}) copy-start(f32[1024,256]{1,0:T(8,128)} %param.9) | copy-start | bytes 3145732
  746.0 91.5 %collective-permute-start.3 = (f32[4096,256]{1,0:T(8,128)S(1)}, f32[4096,256]{1,0:T(8,128)}, u32[]{:S(2)}, u32[]{:S(2)}) collective-permute-start(f32[4096,256]{1,0:T(8,128)S(1)} %add_multiply_fusion), channel_id=1, source_target_pairs={{0,16},{8,24},{16,0},{24,8},{32,48},{40,56},{48,32},{56,40},{64,80... | collective-permute-start | bytes 12582920 | tf_op jit(solution)/shard_map/ppermute | solution.py:18
Sparse Core Ops, SparseCore 0:
  837.6 124.3 reduce-scatter.1
where the time goes:
time: 976 us; the launch traced here: 971 us
  waiting for transfers between devices  319 us (33%)
  other arithmetic  278 us (28%)
  blocking collectives  273 us (28%)
  matrix products  41.4 us (4%)
  local copies, waits for them, and re-layouts  37.3 us (4%)
  between operations  14.9 us (2%)
    psum x4, blocking collectives, on_device(): topic_totals = lax.psum(jnp.sum(topic_panel, axis=0), 'blk')  273 us
    ppermute x4, waiting for transfers between devices, partner(): return lax.ppermute(value, axis, pairs)  195 us
    add x4, other arithmetic, on_device(): (1.0 - step_weight) * topic_panel  131 us
    reduce_scatter x1, waiting for transfers between devices, on_device(): lax.psum_scatter(returned, 'grp', scatter_dimension=0, tiled=True) / groups  125 us
    convert_element_type x4, other arithmetic, on_device(): jnp.exp(lax.digamma(topic_panel) - lax.digamma(topic_totals)[None, :])  124 us
    dot_general x12, matrix products, update_padded(): jnp.einsum('rsdw,rswk->rdk', count_ratio, word_tiles, preferred_element_t...  22.8 us
    reshape x4, local copies, waits for them, and re-layouts, update_padded(): accumulated.reshape(beta_exp.shape)  19.6 us
  transfers between devices with their start and end apart: 5, of which 5 were waited for; matrix products, arithmetic and copies ran while one was open for 0% of the time, Pallas kernels for 0%

commit v1 on v0

v1 whole, which is shorter than its diff:
```python
import jax
import jax.numpy as jnp
from jax import lax
from jax.experimental import pallas as pl
from jax.experimental.pallas import tpu as pltpu
from jax.sharding import PartitionSpec as P

STRATA = 4
LOCAL = 3
ORDER = (0, 1, 3, 2)
SLOTS = 6
TILE = 128
HALF = 64
TOPICS = 256
COLS = 32
VOCAB = 131072
GROUPS = 8
WORD_PRIOR = 0.05
NX, NZ, NY = 4, 4, 4
MESH = pl.DeviceIdType.MESH
NT = (((1,), (1,)), ((), ()))
TN = (((0,), (0,)), ((), ()))
FWD_F, UNM_F, FWD_K, MRG_F, UNM_K, MRG_K, ACROSS = range(7)


def flip(value, bits):
    if bits & 1:
        value = value + 1 - 2 * (value % 2)
    if bits & 2:
        value = value + 2 - 4 * ((value // 2) % 2)
    return value


def psi_parts(x):
    q = x * (x + 3.0)
    d = q * (q + 2.0)
    v = x + 3.5
    r = 1.0 / (v * d)
    rv = r * d
    second = (2.0 * x + 3.0) * (2.0 * q + 2.0) * (r * v)
    r2 = rv * rv
    first = v + rv * (1.0 / 24.0 + r2 * (-37.0 / 5760.0 + r2 * (10313.0 / 2903040.0)))
    return first, second


def psi_parts_wide(x):
    q = x * (x + 3.0)
    v = x + 3.5
    rv = 1.0 / v
    second = (2.0 * x + 3.0) * (2.0 / q) * ((q + 1.0) / (q + 2.0))
    r2 = rv * rv
    first = v + rv * (1.0 / 24.0 + r2 * (-37.0 / 5760.0 + r2 * (10313.0 / 2903040.0)))
    return first, second


def kernel(
    info, inv, lam_any, cnt_any, gam_any, alp_any,
    gout, lout,
    lam, cnt, alp, gbuf, wts, ebuf, beta, theta, ratio, part, ar_src, ar_one, ar_mid, ar_two, rbuf, rrecv,
    lam_sem, in_sem, ar1_s, ar1_r, ar2_s, ar2_r, mv_s, mv_r, rs_s, rs_r,
):
    blk = lax.axis_index("blk")
    grp = lax.axis_index("grp")
    core = blk % 2
    x = (blk // 2) % NX
    z = blk // (2 * NX)
    y = grp % NY
    zh = grp // NY

    def near(k):
        step, side = (k + 1) // 2, (k + 1) % 2
        other = core + 1 - 2 * core if side else core
        return ((z * NX + (x + step) % NX) * 2 + other, grp)

    def far(k):
        return ((((z + k + 1) % NZ) * NX + x) * 2 + core, grp)

    up = (blk, zh * NY + (y + 1) % NY)
    down = (blk, zh * NY + (y + NY - 1) % NY)
    across = (blk, (1 - zh) * NY + y)
    peers = [near(k) for k in range(7)] + [far(k) for k in range(3)] + [up, down, across]

    barrier = pltpu.get_barrier_semaphore()
    for peer in peers:
        pl.semaphore_signal(barrier, inc=1, device_id=peer, device_id_type=MESH)

    chunks = 4
    rows = 2 * COLS // chunks

    def lam_copy(i):
        return pltpu.make_async_copy(lam_any.at[pl.ds(i * rows, rows)], lam.at[pl.ds(i * rows, rows)], lam_sem.at[i])

    for i in range(chunks):
        lam_copy(i).start()
    own = [
        pltpu.make_async_copy(cnt_any.at[0], cnt.at[0], in_sem.at[0]),
        pltpu.make_async_copy(gam_any, gbuf.at[0], in_sem.at[1]),
        pltpu.make_async_copy(alp_any, alp.at[0], in_sem.at[2]),
    ]
    for copy in own:
        copy.start()

    def visit(t):
        return (flip(blk, ORDER[t]), grp)

    def cnt_move(t):
        return pltpu.make_async_remote_copy(cnt_any.at[t], cnt.at[t], mv_s.at[t], mv_r.at[t], device_id=visit(t), device_id_type=MESH)

    def alp_move(t):
        return pltpu.make_async_remote_copy(alp_any, alp.at[t], mv_s.at[4 + t], mv_r.at[4 + t], device_id=visit(t), device_id_type=MESH)

    def gam_move(t):
        bits = ORDER[t] ^ (ORDER[t + 1] if t + 1 < STRATA else 0)
        return pltpu.make_async_remote_copy(gbuf.at[t], gbuf.at[t + 1], mv_s.at[8 + t], mv_r.at[8 + t], device_id=(flip(blk, bits), grp), device_id_type=MESH)

    def one_copy(r, k):
        return pltpu.make_async_remote_copy(ar_src.at[r], ar_one.at[r, k], ar1_s.at[r, k], ar1_r.at[r, k], device_id=near(k), device_id_type=MESH)

    def two_copy(r, k):
        return pltpu.make_async_remote_copy(ar_mid.at[r], ar_two.at[r, k], ar2_s.at[r, k], ar2_r.at[r, k], device_id=far(k), device_id_type=MESH)

    def sum_start(r, value):
        ar_src[r] = value
        for k in range(7):
            one_copy(r, k).start()

    def sum_middle(r):
        total = ar_src[r]
        for k in range(7):
            one_copy(r, k).wait_recv()
            total = total + ar_one[r, k]
        ar_mid[r] = total
        for k in range(3):
            two_copy(r, k).start()

    def sum_end(r):
        total = ar_mid[r]
        for k in range(3):
            two_copy(r, k).wait_recv()
            total = total + ar_two[r, k]
        return total

    def exp_psi(t):
        decay = 0.5**t
        offset = WORD_PRIOR * (1.0 - decay)

        def tile_half(i, carry):
            c = info[t, i // 2]
            h = i % 2
            value = lam[c * 2 + h]
            for s in range(t):
                value = value + part[(s * (SLOTS + 1) + inv[s, c]) * 2 + h]
            first, second = psi_parts(value * decay + offset)
            ebuf[i] = first * jnp.exp(-second)
            return carry

        lax.fori_loop(0, 2 * SLOTS, tile_half, 0)

    def weigh(t):
        live = info[t, SLOTS]
        for j in range(SLOTS):
            keep = jnp.where(j < live, 1.0, 0.0).astype(jnp.float32)
            wts[j // 2, :, (j % 2) * TILE : (j % 2 + 1) * TILE] = cnt[t, j].astype(jnp.float32) * keep

    def scale_beta(totals):
        v = totals - 0.5
        scale = 1.0 / (v + (1.0 / 24.0) / v)
        for i in range(2 * SLOTS):
            beta[i // 4, (i % 4) * HALF : (i % 4 + 1) * HALF, :] = (ebuf[i] * scale).astype(jnp.bfloat16)

    def expect(t):
        for h in range(2):
            g = gbuf[t, h * HALF : (h + 1) * HALF, :]
            first, second = psi_parts(g)
            row_first, row_second = psi_parts_wide(jnp.sum(g, axis=1, keepdims=True))
            theta[h * HALF : (h + 1) * HALF, :] = (
                first * (1.0 / row_first) * jnp.exp(row_second - second)
            ).astype(jnp.bfloat16)
        th = theta[...]
        for p in range(3):
            denom = lax.dot_general(th, beta[p], NT, preferred_element_type=jnp.float32)
            ratio[p] = (wts[p] / denom).astype(jnp.bfloat16)

    def update(t):
        expect(t)
        contrib = jnp.dot(ratio[0], beta[0], preferred_element_type=jnp.float32)
        contrib = contrib + jnp.dot(ratio[1], beta[1], preferred_element_type=jnp.float32)
        contrib = contrib + jnp.dot(ratio[2], beta[2], preferred_element_type=jnp.float32)
        gbuf[t] = alp[t] + theta[...].astype(jnp.float32) * contrib

    def statistics(t):
        expect(t)
        th = theta[...]
        scale = float(2 ** (t + 3))
        total = jnp.zeros((HALF, TOPICS), jnp.float32)
        for p in range(3):
            stat = lax.dot_general(ratio[p], th, TN, preferred_element_type=jnp.float32)
            for i in range(4):
                piece = beta[p, i * HALF : (i + 1) * HALF, :].astype(jnp.float32) * stat[i * HALF : (i + 1) * HALF, :]
                piece = piece.astype(jnp.bfloat16).astype(jnp.float32)
                total = total + piece
                part[(t * (SLOTS + 1)) * 2 + p * 4 + i] = piece * scale
        return jnp.sum(total, axis=0, keepdims=True)

    acc = jnp.zeros((32, TOPICS), jnp.float32)
    for i in range(chunks):
        lam_copy(i).wait()

        def add_rows(n, acc, i=i):
            value = lam[i * rows + n]
            return acc + (value[:32] + value[32:])

        acc = lax.fori_loop(0, rows, add_rows, acc)
    zero = jnp.zeros((HALF, TOPICS), jnp.float32)
    for s in range(STRATA):
        for h in range(2):
            part[(s * (SLOTS + 1) + SLOTS) * 2 + h] = zero
    pl.semaphore_wait(barrier, len(peers))
    sum_start(0, jnp.sum(acc, axis=0, keepdims=True))
    for copy in own:
        copy.wait()
    exp_psi(0)
    sum_middle(0)
    for t in range(1, STRATA):
        cnt_move(t).start()
        alp_move(t).start()
    weigh(0)
    totals = sum_end(0)

    for t in range(STRATA):
        scale_beta(totals)
        lax.fori_loop(0, LOCAL, lambda n, carry, t=t: (update(t), carry)[1], 0)
        gam_move(t).start()
        sums = statistics(t)
        if t + 1 < STRATA:
            sum_start(t + 1, sums)
            exp_psi(t + 1)
            sum_middle(t + 1)
            cnt_move(t + 1).wait_recv()
            alp_move(t + 1).wait_recv()
            weigh(t + 1)
            gam_move(t).wait_recv()
            totals = 0.5 * totals + 0.5 * (WORD_PRIOR * VOCAB + GROUPS * sum_end(t + 1))

    give = 1 - zh
    keep = zh
    ups = (FWD_F, MRG_F, UNM_K)

    def rs_copy(kind, i):
        to = across if kind == ACROSS else up if kind in ups else down
        return pltpu.make_async_remote_copy(rbuf.at[kind, i], rrecv.at[kind, i], rs_s.at[kind, i], rs_r.at[kind, i], device_id=to, device_id_type=MESH)

    def gathered(side, step, i, h):
        c = side * 16 + ((y + step) % NY) * 4 + i
        value = part[inv[0, c] * 2 + h]
        for s in range(1, STRATA):
            value = value + part[(s * (SLOTS + 1) + inv[s, c]) * 2 + h]
        return value

    def each(body):
        lax.fori_loop(0, 4, lambda i, carry: (body(i), carry)[1], 0)

    def put(kind, i, side, step, received=()):
        for other in received:
            rs_copy(other, i).wait_recv()
        for h in range(2):
            part_rows = pl.ds(h * HALF, HALF)
            value = gathered(side, step, i, h)
            for other in received:
                value = value + rrecv[other, i, part_rows, :]
            rbuf[kind, i, part_rows, :] = value
        rs_copy(kind, i).start()

    def first_round(i):
        put(FWD_F, i, give, 2)
        put(UNM_F, i, give, 3)

    def last_round(i):
        for kind in (UNM_K, MRG_K, ACROSS):
            rs_copy(kind, i).wait_recv()
        for h in range(2):
            part_rows = pl.ds(h * HALF, HALF)
            value = gathered(keep, 0, i, h)
            for kind in (UNM_K, MRG_K, ACROSS):
                value = value + rrecv[kind, i, part_rows, :]
            start = lam[(grp * 4 + i) * 2 + h]
            lout[i, part_rows, :] = start * 0.0625 + (value * (1.0 / 128.0) + WORD_PRIOR * 0.9375)

    def middle_round(i):
        put(ACROSS, i, give, 0, (UNM_F, MRG_F))
        put(MRG_K, i, keep, 3, (FWD_K,))

    each(first_round)
    each(lambda i: put(FWD_K, i, keep, 2))
    each(lambda i: put(MRG_F, i, give, 1, (FWD_F,)))
    each(lambda i: put(UNM_K, i, keep, 1))
    each(middle_round)
    gam_move(STRATA - 1).wait_recv()
    gout[...] = gbuf[STRATA]
    each(last_round)

    for r in range(STRATA):
        for k in range(7):
            one_copy(r, k).wait_send()
        for k in range(3):
            two_copy(r, k).wait_send()
        gam_move(r).wait_send()
        if r > 0:
            cnt_move(r).wait_send()
            alp_move(r).wait_send()

    def drain(i):
        for kind in range(7):
            rs_copy(kind, i).wait_send()

    each(drain)


def on_device(lambda_init, gamma_init, dmr_table, features, counts, tile_cols, live_slots):
    doc_alpha = jnp.exp(jnp.sum(jnp.take(dmr_table, features, axis=0), axis=1))
    own = jnp.concatenate([tile_cols[0], live_slots[0][:, None], jnp.zeros((STRATA, 1), jnp.int32)], axis=1)
    blocks = range(lax.axis_size("blk"))
    rows = [own[0:1]] + [
        lax.ppermute(own[t : t + 1], "blk", [(d, d ^ ORDER[t]) for d in blocks]) for t in range(1, STRATA)
    ]
    info = jnp.concatenate(rows, axis=0)
    match = info[:, None, :SLOTS] == jnp.arange(COLS, dtype=jnp.int32)[None, :, None]
    inv = SLOTS + jnp.sum(jnp.where(match, jnp.arange(SLOTS, dtype=jnp.int32) - SLOTS, 0), axis=2)
    inv = inv.astype(jnp.int32)
    smem = pl.BlockSpec(memory_space=pltpu.SMEM)
    hbm = pl.BlockSpec(memory_space=pl.ANY)
    vmem = pl.BlockSpec(memory_space=pltpu.VMEM)
    f32, bf16 = jnp.float32, jnp.bfloat16
    dma = pltpu.SemaphoreType.DMA
    doc = (TILE, TOPICS)
    gamma_out, lambda_out = pl.pallas_call(
        kernel,
        out_shape=(jax.ShapeDtypeStruct(doc, f32), jax.ShapeDtypeStruct((4,) + doc, f32)),
        in_specs=[smem, smem, hbm, hbm, hbm, hbm],
        out_specs=(vmem, vmem),
        scratch_shapes=[
            pltpu.VMEM((2 * COLS, HALF, TOPICS), f32),
            pltpu.VMEM((STRATA, SLOTS, TILE, TILE), jnp.int32),
            pltpu.VMEM((STRATA,) + doc, f32),
            pltpu.VMEM((STRATA + 1,) + doc, f32),
            pltpu.VMEM((3, TILE, 2 * TILE), f32),
            pltpu.VMEM((2 * SLOTS, HALF, TOPICS), f32),
            pltpu.VMEM((3, 2 * TILE, TOPICS), bf16),
            pltpu.VMEM(doc, bf16),
            pltpu.VMEM((3, TILE, 2 * TILE), bf16),
            pltpu.VMEM((STRATA * (SLOTS + 1) * 2, HALF, TOPICS), f32),
            pltpu.VMEM((STRATA, 1, TOPICS), f32),
            pltpu.VMEM((STRATA, 7, 1, TOPICS), f32),
            pltpu.VMEM((STRATA, 1, TOPICS), f32),
            pltpu.VMEM((STRATA, 3, 1, TOPICS), f32),
            pltpu.VMEM((7, 4) + doc, f32),
            pltpu.VMEM((7, 4) + doc, f32),
            dma((4,)),
            dma((3,)),
            dma((STRATA, 7)),
            dma((STRATA, 7)),
            dma((STRATA, 3)),
            dma((STRATA, 3)),
            dma((12,)),
            dma((12,)),
            dma((7, 4)),
            dma((7, 4)),
        ],
        compiler_params=pltpu.CompilerParams(collective_id=0, has_side_effects=True),
        name="strata",
    )(
        info,
        inv,
        lambda_init.reshape(2 * COLS, HALF, TOPICS),
        counts[0],
        gamma_init,
        doc_alpha,
    )
    return gamma_out, lambda_out.reshape(4 * TILE, TOPICS)


def solution(mesh):
    placed = (
        P("blk", None),
        P(("blk", "grp"), None),
        P(),
        P(("blk", "grp"), None),
        P(("blk", "grp"), None, None, None, None),
        P(("blk", "grp"), None, None),
        P(("blk", "grp"), None),
    )
    return jax.shard_map(
        on_device,
        mesh=mesh,
        in_specs=placed,
        out_specs=(P(("blk", "grp"), None), P(("blk", "grp"), None)),
        check_vma=False,
    )
```

time: 976 us -> 118 us (0.12)
  the two profiles are of different devices: /device:TPU:1 before, /device:TPU:2 now
where the time goes in v1:
time: 118 us
  Pallas kernels  104 us (88%)
  local copies, waits for them, and re-layouts  7.2 us (6%)
  other arithmetic  3.23 us (3%)
  starting transfers between devices  2.5 us (2%)
    pallas_call x1, Pallas kernels, on_device(): pl.pallas_call(kernel, out_shape=(jax.ShapeDtypeStruct(doc, f32), jax.Sha...  104 us
    unnamed x6, local copies, waits for them, and re-layouts  3.45 us
    ppermute x3, starting transfers between devices, on_device(): lax.ppermute(own[t:t + 1], 'blk', [(d, d ^ ORDER[t]) for d in blocks])  2.5 us
  transfers between devices with their start and end apart: 3, of which 0 were waited for; matrix products, arithmetic and copies ran while one was open for 4% of the time, Pallas kernels for 0%

profile of v1, /device:TPU:2, one launch (start us, length us, event | category | flops | bytes accessed | tf_op | source)
XLA Modules:
  0.0 118.1 jit_solution(8304419982705755561)
XLA Ops:
  0.6 0.0 copy-start
  0.6 0.1 pad.6.clone
  0.7 0.8 copy.14
  1.5 0.8 add_add_fusion
  2.3 2.3 %collective-permute-start.2 = (s32[1,8]{1,0:T(1,128)S(1)}, s32[1,8]{1,0:T(1,128)S(1)}, u32[]{:S(2)}, u32[]{:S(2)}) collective-permute-start(s32[1,8]{1,0:T(1,128)S(1)} %get-tuple-element.7), channel_id=1, source_target_pairs={{0,16},{8,24},{16,0},{24,8},{32,48},{40,56},{48,32},{56,40},{64,80... | collective-permute-start | bytes 104 | tf_op jit(solution)/shard_map/ppermute | solution.py:324
  4.6 0.0 collective-permute-start.1
  4.6 0.2 collective-permute-start
  4.8 0.7 compare_and_fusion
  5.5 0.7 compare_select_fusion
  6.2 0.1 copy.16
  6.3 0.1 copy.17
  6.4 0.1 reshape.20
  6.6 0.0 copy-done
  6.6 1.6 %gather_fusion = f32[512,256]{1,0:T(8,128)S(1)} fusion(f32[1024,256]{1,0:T(8,128)S(1)} %copy-done, s32[1024]{0:T(1024)S(1)} %pad_clamp_fusion), kind=kCustom, calls=%fused_computation | custom fusion | bytes 1050624 | tf_op jit(solution)/shard_map/jit(_take)/gather | solution.py:320
  8.1 0.1 reshape.19
  8.3 0.4 select_reduce_fusion
  8.7 0.7 exp.3.alp_any
  9.4 0.0 collective-permute-done.2
  9.4 0.0 collective-permute-done.1
  9.4 0.0 collective-permute-done
  9.4 0.0 copy-start.1
  9.4 0.1 copy.15
  9.5 0.1 select_reduce_fusion.1
  9.6 0.6 broadcast_add_fusion.inv
  10.2 0.0 copy-done.1
  10.2 104.5 %strata.1 = (f32[128,256]{1,0:T(8,128)}, f32[4,128,256]{2,1,0:T(8,128)}) custom-call(s32[4,8]{1,0:T(4,128)} %copy-done.1, s32[4,32]{1,0:T(4,128)} %broadcast_add_fusion.inv, f32[64,64,256]{2,1,0:T(8,128)} %bitcast.7, s32[4,6,128,128]{3,2,1,0:T(8,128)} %bitcast.8, f32[128,256]{1,0:T(8,128)} %gam_any.1, f32[128,256]{1,0:T(8,128)} %exp.3.alp_any), custom_call_target="tpu_custom_call" | custom-call | tf_op jit(solution)/shard_map/strata/pallas_call | solution.py:336
  114.7 1.6 %copy.20 = f32[128,256]{1,0:T(8,128)} copy(f32[128,256]{1,0:T(8,128)} %get-tuple-element.12) | data formatting | bytes 262144
  116.2 1.9 %copy.21 = f32[512,256]{1,0:T(8,128)} copy(f32[512,256]{1,0:T(8,128)} %bitcast.9) | data formatting | bytes 1048576
  (4 shorter events, 0.0 us)
Async XLA Ops:
  0.6 5.9 %copy-start = (f32[1024,256]{1,0:T(8,128)S(1)}, f32[1024,256]{1,0:T(8,128)}, u32[]{:S(2)}) copy-start(f32[1024,256]{1,0:T(8,128)} %param.9) | copy-start | bytes 3145732
  2.3 7.1 %collective-permute-start.2 = (s32[1,8]{1,0:T(1,128)S(1)}, s32[1,8]{1,0:T(1,128)S(1)}, u32[]{:S(2)}, u32[]{:S(2)}) collective-permute-start(s32[1,8]{1,0:T(1,128)S(1)} %get-tuple-element.7), channel_id=1, source_target_pairs={{0,16},{8,24},{16,0},{24,8},{32,48},{40,56},{48,32},{56,40},{64,80... | collective-permute-start | bytes 104 | tf_op jit(solution)/shard_map/ppermute | solution.py:324
  4.6 4.8 %collective-permute-start.1 = (s32[1,8]{1,0:T(1,128)S(1)}, s32[1,8]{1,0:T(1,128)S(1)}, u32[]{:S(2)}, u32[]{:S(2)}) collective-permute-start(s32[1,8]{1,0:T(1,128)S(1)} %get-tuple-element.8), channel_id=1, source_target_pairs={{0,24},{8,16},{16,8},{24,0},{32,56},{40,48},{48,40},{56,32},{64,88... | collective-permute-start | bytes 104 | tf_op jit(solution)/shard_map/ppermute | solution.py:324
  4.6 4.8 %collective-permute-start = (s32[1,8]{1,0:T(1,128)S(1)}, s32[1,8]{1,0:T(1,128)S(1)}, u32[]{:S(2)}, u32[]{:S(2)}) collective-permute-start(s32[1,8]{1,0:T(1,128)S(1)} %get-tuple-element.9), channel_id=1, source_target_pairs={{0,8},{8,0},{16,24},{24,16},{32,40},{40,32},{48,56},{56,48},{64,72... | collective-permute-start | bytes 104 | tf_op jit(solution)/shard_map/ppermute | solution.py:324
  9.4 0.8 copy-start.1

commit v2 on v1

--- a/solution.py
+++ b/solution.py
@@ -54,10 +54,11 @@
 
 
 def kernel(
-    info, inv, lam_any, cnt_any, gam_any, alp_any,
+    lam_any, cnt_any, gam_any, tab_any, feat_any, cols_any, live_any,
     gout, lout,
-    lam, cnt, alp, gbuf, wts, ebuf, beta, theta, ratio, part, ar_src, ar_one, ar_mid, ar_two, rbuf, rrecv,
-    lam_sem, in_sem, ar1_s, ar1_r, ar2_s, ar2_r, mv_s, mv_r, rs_s, rs_r,
+    lam, tab, cnt, alp, gbuf, wts, ebuf, beta, theta, ratio, part, colv, livv, feat, cols, live, inv,
+    ar_src, ar_one, ar_mid, ar_two, rbuf, rrecv,
+    lam_sem, in_sem, id_s, id_r, ar1_s, ar1_r, ar2_s, ar2_r, mv_s, mv_r, rs_s, rs_r,
 ):
     blk = lax.axis_index("blk")
     grp = lax.axis_index("grp")
@@ -75,6 +76,9 @@
     def far(k):
         return ((((z + k + 1) % NZ) * NX + x) * 2 + core, grp)
 
+    def flipped(bits):
+        return (flip(blk, bits), grp)
+
     up = (blk, zh * NY + (y + 1) % NY)
     down = (blk, zh * NY + (y + NY - 1) % NY)
     across = (blk, (1 - zh) * NY + y)
@@ -90,28 +94,44 @@
     def lam_copy(i):
         return pltpu.make_async_copy(lam_any.at[pl.ds(i * rows, rows)], lam.at[pl.ds(i * rows, rows)], lam_sem.at[i])
 
+    own_ids = [
+        pltpu.make_async_copy(cols_any, cols.at[0], in_sem.at[0]),
+        pltpu.make_async_copy(live_any, live.at[0], in_sem.at[1]),
+    ]
+    own_docs = [
+        pltpu.make_async_copy(feat_any, feat, in_sem.at[2]),
+        pltpu.make_async_copy(tab_any, tab, in_sem.at[3]),
+        pltpu.make_async_copy(cnt_any.at[0], cnt.at[0], in_sem.at[4]),
+        pltpu.make_async_copy(gam_any, gbuf.at[0], in_sem.at[5]),
+    ]
+    for copy in own_ids:
+        copy.start()
     for i in range(chunks):
         lam_copy(i).start()
-    own = [
-        pltpu.make_async_copy(cnt_any.at[0], cnt.at[0], in_sem.at[0]),
-        pltpu.make_async_copy(gam_any, gbuf.at[0], in_sem.at[1]),
-        pltpu.make_async_copy(alp_any, alp.at[0], in_sem.at[2]),
-    ]
-    for copy in own:
+    for copy in own_docs:
         copy.start()
 
-    def visit(t):
-        return (flip(blk, ORDER[t]), grp)
-
-    def cnt_move(t):
-        return pltpu.make_async_remote_copy(cnt_any.at[t], cnt.at[t], mv_s.at[t], mv_r.at[t], device_id=visit(t), device_id_type=MESH)
+    def move(src, dst, n, bits):
+        return pltpu.make_async_remote_copy(src, dst, mv_s.at[n], mv_r.at[n], device_id=flipped(bits), device_id_type=MESH)
+
+    def cnt_move(t, second):
+        tiles = pl.ds(4, 2) if second else pl.ds(0, 4)
+        return move(cnt_any.at[t, tiles], cnt.at[t, tiles], 2 * t + second, ORDER[t])
 
     def alp_move(t):
-        return pltpu.make_async_remote_copy(alp_any, alp.at[t], mv_s.at[4 + t], mv_r.at[4 + t], device_id=visit(t), device_id_type=MESH)
+        if t == 3:
+            return move(alp.at[2], alp.at[3], 8 + t, ORDER[2] ^ ORDER[3])
+        return move(alp.at[0], alp.at[t], 8 + t, ORDER[t])
 
     def gam_move(t):
         bits = ORDER[t] ^ (ORDER[t + 1] if t + 1 < STRATA else 0)
-        return pltpu.make_async_remote_copy(gbuf.at[t], gbuf.at[t + 1], mv_s.at[8 + t], mv_r.at[8 + t], device_id=(flip(blk, bits), grp), device_id_type=MESH)
+        return move(gbuf.at[t], gbuf.at[t + 1], 12 + t, bits)
+
+    def id_moves(t):
+        return [
+            pltpu.make_async_remote_copy(cols_any, colv.at[t], id_s.at[t, 0], id_r.at[t, 0], device_id=flipped(ORDER[t]), device_id_type=MESH),
+            pltpu.make_async_remote_copy(live_any, livv.at[t], id_s.at[t, 1], id_r.at[t, 1], device_id=flipped(ORDER[t]), device_id_type=MESH),
+        ]
 
     def one_copy(r, k):
         return pltpu.make_async_remote_copy(ar_src.at[r], ar_one.at[r, k], ar1_s.at[r, k], ar1_r.at[r, k], device_id=near(k), device_id_type=MESH)
@@ -140,12 +160,26 @@
             total = total + ar_two[r, k]
         return total
 
+    def find_slots(s):
+        ids = [cols[s, s, j] for j in range(SLOTS)]
+
+        def column(i, carry):
+            for n in range(4):
+                c = i * 4 + n
+                slot = SLOTS
+                for j in range(SLOTS):
+                    slot = jnp.where(ids[j] == c, j, slot)
+                inv[s, c] = slot
+            return carry
+
+        lax.fori_loop(0, COLS // 4, column, 0)
+
     def exp_psi(t):
         decay = 0.5**t
         offset = WORD_PRIOR * (1.0 - decay)
 
         def tile_half(i, carry):
-            c = info[t, i // 2]
+            c = cols[t, t, i // 2]
             h = i % 2
             value = lam[c * 2 + h]
             for s in range(t):
@@ -157,9 +191,9 @@
         lax.fori_loop(0, 2 * SLOTS, tile_half, 0)
 
     def weigh(t):
-        live = info[t, SLOTS]
+        used = live[t, 0, t]
         for j in range(SLOTS):
-            keep = jnp.where(j < live, 1.0, 0.0).astype(jnp.float32)
+            keep = jnp.where(j < used, 1.0, 0.0).astype(jnp.float32)
             wts[j // 2, :, (j % 2) * TILE : (j % 2 + 1) * TILE] = cnt[t, j].astype(jnp.float32) * keep
 
     def scale_beta(totals):
@@ -167,6 +201,20 @@
         scale = 1.0 / (v + (1.0 / 24.0) / v)
         for i in range(2 * SLOTS):
             beta[i // 4, (i % 4) * HALF : (i % 4 + 1) * HALF, :] = (ebuf[i] * scale).astype(jnp.bfloat16)
+
+    def doc_prior():
+        def eight(b, carry):
+            for r in range(8):
+                n = b * 8 + r
+                value = tab[pl.ds(feat[0, n], 1), :]
+                for f in range(1, 4):
+                    value = value + tab[pl.ds(feat[f, n], 1), :]
+                alp[0, pl.ds(n, 1), :] = value
+            return carry
+
+        lax.fori_loop(0, TILE // 8, eight, 0)
+        for h in range(2):
+            alp[0, h * HALF : (h + 1) * HALF, :] = jnp.exp(alp[0, h * HALF : (h + 1) * HALF, :])
 
     def expect(t):
         for h in range(2):
@@ -176,31 +224,32 @@
             theta[h * HALF : (h + 1) * HALF, :] = (
                 first * (1.0 / row_first) * jnp.exp(row_second - second)
             ).astype(jnp.bfloat16)
+
+    def divide():
         th = theta[...]
         for p in range(3):
             denom = lax.dot_general(th, beta[p], NT, preferred_element_type=jnp.float32)
             ratio[p] = (wts[p] / denom).astype(jnp.bfloat16)
 
+    def contribution():
+        value = jnp.dot(ratio[0], beta[0], preferred_element_type=jnp.float32)
+        value = value + jnp.dot(ratio[1], beta[1], preferred_element_type=jnp.float32)
+        value = value + jnp.dot(ratio[2], beta[2], preferred_element_type=jnp.float32)
+        return theta[...].astype(jnp.float32) * value
+
     def update(t):
+        divide()
+        gbuf[t] = alp[t] + contribution()
         expect(t)
-        contrib = jnp.dot(ratio[0], beta[0], preferred_element_type=jnp.float32)
-        contrib = contrib + jnp.dot(ratio[1], beta[1], preferred_element_type=jnp.float32)
-        contrib = contrib + jnp.dot(ratio[2], beta[2], preferred_element_type=jnp.float32)
-        gbuf[t] = alp[t] + theta[...].astype(jnp.float32) * contrib
 
     def statistics(t):
-        expect(t)
         th = theta[...]
         scale = float(2 ** (t + 3))
-        total = jnp.zeros((HALF, TOPICS), jnp.float32)
         for p in range(3):
             stat = lax.dot_general(ratio[p], th, TN, preferred_element_type=jnp.float32)
             for i in range(4):
                 piece = beta[p, i * HALF : (i + 1) * HALF, :].astype(jnp.float32) * stat[i * HALF : (i + 1) * HALF, :]
-                piece = piece.astype(jnp.bfloat16).astype(jnp.float32)
-                total = total + piece
-                part[(t * (SLOTS + 1)) * 2 + p * 4 + i] = piece * scale
-        return jnp.sum(total, axis=0, keepdims=True)
+                part[(t * (SLOTS + 1)) * 2 + p * 4 + i] = piece.astype(jnp.bfloat16).astype(jnp.float32) * scale
 
     acc = jnp.zeros((32, TOPICS), jnp.float32)
     for i in range(chunks):
@@ -211,35 +260,73 @@
             return acc + (value[:32] + value[32:])
 
         acc = lax.fori_loop(0, rows, add_rows, acc)
+    sums = jnp.sum(acc, axis=0, keepdims=True)
+    for copy in own_ids:
+        copy.wait()
+    pl.semaphore_wait(barrier, len(peers))
+    sum_start(0, sums)
+    for t in range(1, STRATA):
+        for copy in id_moves(t):
+            copy.start()
+    exp_psi(0)
     zero = jnp.zeros((HALF, TOPICS), jnp.float32)
     for s in range(STRATA):
         for h in range(2):
             part[(s * (SLOTS + 1) + SLOTS) * 2 + h] = zero
-    pl.semaphore_wait(barrier, len(peers))
-    sum_start(0, jnp.sum(acc, axis=0, keepdims=True))
-    for copy in own:
+    sum_middle(0)
+    for t in (1, 2):
+        cnt_move(t, 0).start()
+    cnt_move(1, 1).start()
+    for copy in own_docs:
         copy.wait()
-    exp_psi(0)
-    sum_middle(0)
+    expect(0)
+    weigh(0)
+    doc_prior()
+    alp_move(1).start()
+    find_slots(0)
     for t in range(1, STRATA):
-        cnt_move(t).start()
-        alp_move(t).start()
-    weigh(0)
+        for copy in id_moves(t):
+            copy.wait_recv()
+        local = [
+            pltpu.make_async_copy(colv.at[t], cols.at[t], in_sem.at[0]),
+            pltpu.make_async_copy(livv.at[t], live.at[t], in_sem.at[1]),
+        ]
+        for copy in local:
+            copy.start()
+        for copy in local:
+            copy.wait()
     totals = sum_end(0)
 
     for t in range(STRATA):
         scale_beta(totals)
         lax.fori_loop(0, LOCAL, lambda n, carry, t=t: (update(t), carry)[1], 0)
-        gam_move(t).start()
-        sums = statistics(t)
+        if t != 1:
+            gam_move(t).start()
+        divide()
         if t + 1 < STRATA:
-            sum_start(t + 1, sums)
+            sum_start(t + 1, jnp.sum(contribution(), axis=0, keepdims=True))
+        if t == 1:
+            gam_move(t).start()
+        if t == 2:
+            cnt_move(3, 1).start()
+        statistics(t)
+        if t + 1 < STRATA:
             exp_psi(t + 1)
             sum_middle(t + 1)
-            cnt_move(t + 1).wait_recv()
+            if t == 0:
+                cnt_move(2, 1).start()
+                alp_move(2).start()
+            if t == 1:
+                cnt_move(3, 0).start()
+            find_slots(t + 1)
             alp_move(t + 1).wait_recv()
+            if t == 1:
+                alp_move(3).start()
+            gam_move(t).wait_recv()
+            expect(t + 1)
+            cnt_move(t + 1, 0).wait_recv()
+            cnt_move(t + 1, 1).wait_recv()
             weigh(t + 1)
-            gam_move(t).wait_recv()
             totals = 0.5 * totals + 0.5 * (WORD_PRIOR * VOCAB + GROUPS * sum_end(t + 1))
 
     give = 1 - zh
@@ -256,9 +343,6 @@
         for s in range(1, STRATA):
             value = value + part[(s * (SLOTS + 1) + inv[s, c]) * 2 + h]
         return value
-
-    def each(body):
-        lax.fori_loop(0, 4, lambda i, carry: (body(i), carry)[1], 0)
 
     def put(kind, i, side, step, received=()):
         for other in received:
@@ -271,9 +355,44 @@
             rbuf[kind, i, part_rows, :] = value
         rs_copy(kind, i).start()
 
-    def first_round(i):
-        put(FWD_F, i, give, 2)
+    def each(body):
+        lax.fori_loop(0, 4, lambda i, carry: (body(i), carry)[1], 0)
+
+    def pair(first):
+        put(FWD_F, first, give, 2)
+        put(UNM_F, first, give, 3)
+
+    def merge_give(i):
+        put(MRG_F, i, give, 1, (FWD_F,))
+
+    def merge_keep(i):
+        put(MRG_K, i, keep, 3, (FWD_K,))
+
+    def send_across(i):
+        put(ACROSS, i, give, 0, (UNM_F, MRG_F))
+
+    pair(0)
+    pair(1)
+    for i in (2, 3):
         put(UNM_F, i, give, 3)
+    each(lambda i: put(FWD_K, i, keep, 2))
+    merge_give(0)
+    put(FWD_F, 2, give, 2)
+    merge_give(1)
+    put(FWD_F, 3, give, 2)
+    send_across(0)
+    merge_give(2)
+    send_across(1)
+    merge_keep(0)
+    merge_give(3)
+    each(lambda i: put(UNM_K, i, keep, 1))
+    merge_keep(1)
+    send_across(2)
+    merge_keep(2)
+    send_across(3)
+    merge_keep(3)
+    gam_move(STRATA - 1).wait_recv()
+    gout[...] = gbuf[STRATA]
 
     def last_round(i):
         for kind in (UNM_K, MRG_K, ACROSS):
@@ -286,17 +405,6 @@
             start = lam[(grp * 4 + i) * 2 + h]
             lout[i, part_rows, :] = start * 0.0625 + (value * (1.0 / 128.0) + WORD_PRIOR * 0.9375)
 
-    def middle_round(i):
-        put(ACROSS, i, give, 0, (UNM_F, MRG_F))
-        put(MRG_K, i, keep, 3, (FWD_K,))
-
-    each(first_round)
-    each(lambda i: put(FWD_K, i, keep, 2))
-    each(lambda i: put(MRG_F, i, give, 1, (FWD_F,)))
-    each(lambda i: put(UNM_K, i, keep, 1))
-    each(middle_round)
-    gam_move(STRATA - 1).wait_recv()
-    gout[...] = gbuf[STRATA]
     each(last_round)
 
     for r in range(STRATA):
@@ -306,8 +414,11 @@
             two_copy(r, k).wait_send()
         gam_move(r).wait_send()
         if r > 0:
-            cnt_move(r).wait_send()
+            cnt_move(r, 0).wait_send()
+            cnt_move(r, 1).wait_send()
             alp_move(r).wait_send()
+            for copy in id_moves(r):
+                copy.wait_send()
 
     def drain(i):
         for kind in range(7):
@@ -317,30 +428,20 @@
 
 
 def on_device(lambda_init, gamma_init, dmr_table, features, counts, tile_cols, live_slots):
-    doc_alpha = jnp.exp(jnp.sum(jnp.take(dmr_table, features, axis=0), axis=1))
-    own = jnp.concatenate([tile_cols[0], live_slots[0][:, None], jnp.zeros((STRATA, 1), jnp.int32)], axis=1)
-    blocks = range(lax.axis_size("blk"))
-    rows = [own[0:1]] + [
-        lax.ppermute(own[t : t + 1], "blk", [(d, d ^ ORDER[t]) for d in blocks]) for t in range(1, STRATA)
-    ]
-    info = jnp.concatenate(rows, axis=0)
-    match = info[:, None, :SLOTS] == jnp.arange(COLS, dtype=jnp.int32)[None, :, None]
-    inv = SLOTS + jnp.sum(jnp.where(match, jnp.arange(SLOTS, dtype=jnp.int32) - SLOTS, 0), axis=2)
-    inv = inv.astype(jnp.int32)
-    smem = pl.BlockSpec(memory_space=pltpu.SMEM)
     hbm = pl.BlockSpec(memory_space=pl.ANY)
     vmem = pl.BlockSpec(memory_space=pltpu.VMEM)
-    f32, bf16 = jnp.float32, jnp.bfloat16
+    f32, bf16, i32 = jnp.float32, jnp.bfloat16, jnp.int32
     dma = pltpu.SemaphoreType.DMA
     doc = (TILE, TOPICS)
     gamma_out, lambda_out = pl.pallas_call(
         kernel,
-        out_shape=(jax.ShapeDtypeStruct(doc, f32), jax.ShapeDtypeStruct((4,) + doc, f32)),
-        in_specs=[smem, smem, hbm, hbm, hbm, hbm],
+        out_shape=(pltpu.VMEM(doc, f32), pltpu.VMEM((4,) + doc, f32)),
+        in_specs=[hbm] * 7,
         out_specs=(vmem, vmem),
         scratch_shapes=[
             pltpu.VMEM((2 * COLS, HALF, TOPICS), f32),
-            pltpu.VMEM((STRATA, SLOTS, TILE, TILE), jnp.int32),
+            pltpu.VMEM((1024, TOPICS), f32),
+            pltpu.VMEM((STRATA, SLOTS, TILE, TILE), i32),
             pltpu.VMEM((STRATA,) + doc, f32),
             pltpu.VMEM((STRATA + 1,) + doc, f32),
             pltpu.VMEM((3, TILE, 2 * TILE), f32),
@@ -349,6 +450,12 @@
             pltpu.VMEM(doc, bf16),
             pltpu.VMEM((3, TILE, 2 * TILE), bf16),
             pltpu.VMEM((STRATA * (SLOTS + 1) * 2, HALF, TOPICS), f32),
+            pltpu.VMEM((STRATA, STRATA, SLOTS), i32),
+            pltpu.VMEM((STRATA, 1, STRATA), i32),
+            pltpu.SMEM((4, TILE), i32),
+            pltpu.SMEM((STRATA, STRATA, SLOTS), i32),
+            pltpu.SMEM((STRATA, 1, STRATA), i32),
+            pltpu.SMEM((STRATA, COLS), i32),
             pltpu.VMEM((STRATA, 1, TOPICS), f32),
             pltpu.VMEM((STRATA, 7, 1, TOPICS), f32),
             pltpu.VMEM((STRATA, 1, TOPICS), f32),
@@ -356,25 +463,28 @@
             pltpu.VMEM((7, 4) + doc, f32),
             pltpu.VMEM((7, 4) + doc, f32),
             dma((4,)),
-            dma((3,)),
+            dma((6,)),
+            dma((STRATA, 2)),
+            dma((STRATA, 2)),
             dma((STRATA, 7)),
             dma((STRATA, 7)),
             dma((STRATA, 3)),
             dma((STRATA, 3)),
-            dma((12,)),
-            dma((12,)),
+            dma((16,)),
+            dma((16,)),
             dma((7, 4)),
             dma((7, 4)),
         ],
         compiler_params=pltpu.CompilerParams(collective_id=0, has_side_effects=True),
         name="strata",
     )(
-        info,
-        inv,
         lambda_init.reshape(2 * COLS, HALF, TOPICS),
         counts[0],
         gamma_init,
-        doc_alpha,
+        dmr_table,
+        features.T,
+        tile_cols[0],
+        live_slots,
     )
     return gamma_out, lambda_out.reshape(4 * TILE, TOPICS)
 

time: 118 us -> 85.4 us (0.72)
  the two profiles are of different devices: /device:TPU:2 before, /device:TPU:1 now
where the time goes in v2:
time: 85.4 us; the launch traced here: 85.3 us
  Pallas kernels  83.2 us (97%)
  local copies, waits for them, and re-layouts  1.45 us (2%)
    pallas_call x1, Pallas kernels, on_device(): pl.pallas_call(kernel, out_shape=(pltpu.VMEM(doc, f32), pltpu.VMEM((4,) +...  83.2 us

profile of v2, /device:TPU:1, one launch (start us, length us, event | category | flops | bytes accessed | tf_op | source)
XLA Modules:
  0.0 85.3 jit_solution(6617870455985449003)
XLA Ops:
  0.6 83.2 %strata.1 = (f32[128,256]{1,0:T(8,128)S(1)}, f32[4,128,256]{2,1,0:T(8,128)S(1)}) custom-call(f32[64,64,256]{2,1,0:T(8,128)} %bitcast.6, s32[4,6,128,128]{3,2,1,0:T(8,128)} %bitcast.7, f32[128,256]{1,0:T(8,128)} %gam_any.1, f32[1024,256]{1,0:T(8,128)} %tab_any.1, s32[4,128]{1,0:T(4,128)} %bitcast.8, s32[4,6]{1,0:T(4,128)} %bitcast.9, s32[1,4]{1,0:T(1,128)} %live_any.1), custom_call_target="tpu_custom_call" | custom-call | tf_op jit(solution)/shard_map/strata/pallas_call | solution.py:436
  83.8 0.7 copy.11
  84.5 0.8 copy.12

commit v3 on v2

--- a/solution.py
+++ b/solution.py
@@ -20,7 +20,9 @@
 MESH = pl.DeviceIdType.MESH
 NT = (((1,), (1,)), ((), ()))
 TN = (((0,), (0,)), ((), ()))
+PIECES = ((), ((0, 6),), ((0, 5), (5, 1)), ((0, 3), (3, 3)))
 FWD_F, UNM_F, FWD_K, MRG_F, UNM_K, MRG_K, ACROSS = range(7)
+FAR_FIRST = sorted(range(1, 2 * NX * NZ), key=lambda k: -(min(k // 2 % NX, NX - k // 2 % NX) + min(k // (2 * NX), NZ - k // (2 * NX))))
 
 
 def flip(value, bits):
@@ -56,9 +58,9 @@
 def kernel(
     lam_any, cnt_any, gam_any, tab_any, feat_any, cols_any, live_any,
     gout, lout,
-    lam, tab, cnt, alp, gbuf, wts, ebuf, beta, theta, ratio, part, colv, livv, feat, cols, live, inv,
-    ar_src, ar_one, ar_mid, ar_two, rbuf, rrecv,
-    lam_sem, in_sem, id_s, id_r, ar1_s, ar1_r, ar2_s, ar2_r, mv_s, mv_r, rs_s, rs_r,
+    lam, tab, cnt, alp, gbuf, wts, ebuf, beta, theta, ratio, part, colv, livv, featv, feat, cols, live, inv,
+    ar_src, ar_dst, rbuf, rrecv,
+    lam_sem, in_sem, id_s, id_r, ar_s, ar_r, mv_s, mv_r, rs_s, rs_r,
 ):
     blk = lax.axis_index("blk")
     grp = lax.axis_index("grp")
@@ -68,13 +70,11 @@
     y = grp % NY
     zh = grp // NY
 
-    def near(k):
-        step, side = (k + 1) // 2, (k + 1) % 2
-        other = core + 1 - 2 * core if side else core
-        return ((z * NX + (x + step) % NX) * 2 + other, grp)
-
-    def far(k):
-        return ((((z + k + 1) % NZ) * NX + x) * 2 + core, grp)
+    def other(k):
+        side = core + 1 - 2 * core if k % 2 else core
+        return ((((z + k // (2 * NX)) % NZ) * NX + (x + (k // 2) % NX) % NX) * 2 + side, grp)
+
+    others = [other(k) for k in FAR_FIRST]
 
     def flipped(bits):
         return (flip(blk, bits), grp)
@@ -82,7 +82,7 @@
     up = (blk, zh * NY + (y + 1) % NY)
     down = (blk, zh * NY + (y + NY - 1) % NY)
     across = (blk, (1 - zh) * NY + y)
-    peers = [near(k) for k in range(7)] + [far(k) for k in range(3)] + [up, down, across]
+    peers = others + [up, down, across]
 
     barrier = pltpu.get_barrier_semaphore()
     for peer in peers:
@@ -114,14 +114,15 @@
     def move(src, dst, n, bits):
         return pltpu.make_async_remote_copy(src, dst, mv_s.at[n], mv_r.at[n], device_id=flipped(bits), device_id_type=MESH)
 
-    def cnt_move(t, second):
-        tiles = pl.ds(4, 2) if second else pl.ds(0, 4)
-        return move(cnt_any.at[t, tiles], cnt.at[t, tiles], 2 * t + second, ORDER[t])
+    def cnt_move(t, n):
+        tiles = pl.ds(*PIECES[t][n])
+        return move(cnt_any.at[t, tiles], cnt.at[t, tiles], 3 * (t - 1) + n, ORDER[t])
 
     def alp_move(t):
-        if t == 3:
-            return move(alp.at[2], alp.at[3], 8 + t, ORDER[2] ^ ORDER[3])
-        return move(alp.at[0], alp.at[t], 8 + t, ORDER[t])
+        return move(alp.at[t - 1], alp.at[t], 8 + t, ORDER[t - 1] ^ ORDER[t])
+
+    def feat_move():
+        return move(feat_any, featv, 10, ORDER[2])
 
     def gam_move(t):
         bits = ORDER[t] ^ (ORDER[t + 1] if t + 1 < STRATA else 0)
@@ -133,32 +134,20 @@
             pltpu.make_async_remote_copy(live_any, livv.at[t], id_s.at[t, 1], id_r.at[t, 1], device_id=flipped(ORDER[t]), device_id_type=MESH),
         ]
 
-    def one_copy(r, k):
-        return pltpu.make_async_remote_copy(ar_src.at[r], ar_one.at[r, k], ar1_s.at[r, k], ar1_r.at[r, k], device_id=near(k), device_id_type=MESH)
-
-    def two_copy(r, k):
-        return pltpu.make_async_remote_copy(ar_mid.at[r], ar_two.at[r, k], ar2_s.at[r, k], ar2_r.at[r, k], device_id=far(k), device_id_type=MESH)
-
     def sum_start(r, value):
         ar_src[r] = value
-        for k in range(7):
-            one_copy(r, k).start()
-
-    def sum_middle(r):
-        total = ar_src[r]
-        for k in range(7):
-            one_copy(r, k).wait_recv()
-            total = total + ar_one[r, k]
-        ar_mid[r] = total
-        for k in range(3):
-            two_copy(r, k).start()
+        for k, peer in enumerate(others):
+            pltpu.make_async_remote_copy(ar_src.at[r], ar_dst.at[r, k], ar_s.at[r], ar_r.at[r], device_id=peer, device_id_type=MESH).start()
+
+    def sum_wait(r, sem):
+        pltpu.make_async_copy(ar_dst.at[r], ar_dst.at[r], sem.at[r]).wait()
 
     def sum_end(r):
-        total = ar_mid[r]
-        for k in range(3):
-            two_copy(r, k).wait_recv()
-            total = total + ar_two[r, k]
-        return total
+        sum_wait(r, ar_r)
+        parts = [ar_src[r]] + [ar_dst[r, k] for k in range(len(others))]
+        while len(parts) > 1:
+            parts = [sum(parts[i + 1 : i + 2], parts[i]) for i in range(0, len(parts), 2)]
+        return parts[0]
 
     def find_slots(s):
         ids = [cols[s, s, j] for j in range(SLOTS)]
@@ -202,19 +191,19 @@
         for i in range(2 * SLOTS):
             beta[i // 4, (i % 4) * HALF : (i % 4 + 1) * HALF, :] = (ebuf[i] * scale).astype(jnp.bfloat16)
 
-    def doc_prior():
+    def doc_prior(t):
         def eight(b, carry):
             for r in range(8):
                 n = b * 8 + r
                 value = tab[pl.ds(feat[0, n], 1), :]
                 for f in range(1, 4):
                     value = value + tab[pl.ds(feat[f, n], 1), :]
-                alp[0, pl.ds(n, 1), :] = value
+                alp[t, pl.ds(n, 1), :] = value
             return carry
 
         lax.fori_loop(0, TILE // 8, eight, 0)
         for h in range(2):
-            alp[0, h * HALF : (h + 1) * HALF, :] = jnp.exp(alp[0, h * HALF : (h + 1) * HALF, :])
+            alp[t, h * HALF : (h + 1) * HALF, :] = jnp.exp(alp[t, h * HALF : (h + 1) * HALF, :])
 
     def expect(t):
         for h in range(2):
@@ -268,21 +257,23 @@
     for t in range(1, STRATA):
         for copy in id_moves(t):
             copy.start()
+    feat_move().start()
+    cnt_move(2, 0).start()
+    cnt_move(1, 0).start()
     exp_psi(0)
     zero = jnp.zeros((HALF, TOPICS), jnp.float32)
     for s in range(STRATA):
         for h in range(2):
             part[(s * (SLOTS + 1) + SLOTS) * 2 + h] = zero
-    sum_middle(0)
-    for t in (1, 2):
-        cnt_move(t, 0).start()
-    cnt_move(1, 1).start()
     for copy in own_docs:
         copy.wait()
     expect(0)
     weigh(0)
-    doc_prior()
+    doc_prior(0)
     alp_move(1).start()
+    feat_move().wait_recv()
+    next_feat = pltpu.make_async_copy(featv, feat, in_sem.at[2])
+    next_feat.start()
     find_slots(0)
     for t in range(1, STRATA):
         for copy in id_moves(t):
@@ -305,27 +296,26 @@
         divide()
         if t + 1 < STRATA:
             sum_start(t + 1, jnp.sum(contribution(), axis=0, keepdims=True))
+        if t == 0:
+            cnt_move(2, 1).start()
+            cnt_move(3, 0).start()
         if t == 1:
             gam_move(t).start()
-        if t == 2:
             cnt_move(3, 1).start()
         statistics(t)
         if t + 1 < STRATA:
             exp_psi(t + 1)
-            sum_middle(t + 1)
+            find_slots(t + 1)
             if t == 0:
-                cnt_move(2, 1).start()
-                alp_move(2).start()
-            if t == 1:
-                cnt_move(3, 0).start()
-            find_slots(t + 1)
-            alp_move(t + 1).wait_recv()
-            if t == 1:
+                next_feat.wait()
+                doc_prior(2)
                 alp_move(3).start()
+            if t != 1:
+                alp_move(t + 1).wait_recv()
             gam_move(t).wait_recv()
             expect(t + 1)
-            cnt_move(t + 1, 0).wait_recv()
-            cnt_move(t + 1, 1).wait_recv()
+            for n in range(len(PIECES[t + 1])):
+                cnt_move(t + 1, n).wait_recv()
             weigh(t + 1)
             totals = 0.5 * totals + 0.5 * (WORD_PRIOR * VOCAB + GROUPS * sum_end(t + 1))
 
@@ -408,15 +398,15 @@
     each(last_round)
 
     for r in range(STRATA):
-        for k in range(7):
-            one_copy(r, k).wait_send()
-        for k in range(3):
-            two_copy(r, k).wait_send()
+        sum_wait(r, ar_s)
         gam_move(r).wait_send()
         if r > 0:
-            cnt_move(r, 0).wait_send()
-            cnt_move(r, 1).wait_send()
-            alp_move(r).wait_send()
+            if r == 2:
+                feat_move().wait_send()
+            else:
+                alp_move(r).wait_send()
+            for n in range(len(PIECES[r])):
+                cnt_move(r, n).wait_send()
             for copy in id_moves(r):
                 copy.wait_send()
 
@@ -452,24 +442,21 @@
             pltpu.VMEM((STRATA * (SLOTS + 1) * 2, HALF, TOPICS), f32),
             pltpu.VMEM((STRATA, STRATA, SLOTS), i32),
             pltpu.VMEM((STRATA, 1, STRATA), i32),
+            pltpu.VMEM((4, TILE), i32),
             pltpu.SMEM((4, TILE), i32),
             pltpu.SMEM((STRATA, STRATA, SLOTS), i32),
             pltpu.SMEM((STRATA, 1, STRATA), i32),
             pltpu.SMEM((STRATA, COLS), i32),
             pltpu.VMEM((STRATA, 1, TOPICS), f32),
-            pltpu.VMEM((STRATA, 7, 1, TOPICS), f32),
-            pltpu.VMEM((STRATA, 1, TOPICS), f32),
-            pltpu.VMEM((STRATA, 3, 1, TOPICS), f32),
+            pltpu.VMEM((STRATA, len(FAR_FIRST), 1, TOPICS), f32),
             pltpu.VMEM((7, 4) + doc, f32),
             pltpu.VMEM((7, 4) + doc, f32),
             dma((4,)),
             dma((6,)),
             dma((STRATA, 2)),
             dma((STRATA, 2)),
-            dma((STRATA, 7)),
-            dma((STRATA, 7)),
-            dma((STRATA, 3)),
-            dma((STRATA, 3)),
+            dma((STRATA,)),
+            dma((STRATA,)),
             dma((16,)),
             dma((16,)),
             dma((7, 4)),

time: 85.4 us -> 81.6 us (0.956)
  Pallas kernels: 83.2 us -> 79.4 us
    pallas_call x1, Pallas kernels: 83.2 us -> 79.4 us  [on_device(): pl.pallas_call(kernel, out_shape=(pltpu.VMEM(doc, f32), pltpu.VMEM((4,) +...]
where the time goes in v3:
time: 81.6 us; the launch traced here: 81.5 us
  Pallas kernels  79.4 us (97%)
  local copies, waits for them, and re-layouts  1.45 us (2%)
    pallas_call x1, Pallas kernels, on_device(): pl.pallas_call(kernel, out_shape=(pltpu.VMEM(doc, f32), pltpu.VMEM((4,) +...  79.4 us

profile of v3, /device:TPU:1, one launch (start us, length us, event | category | flops | bytes accessed | tf_op | source)
XLA Modules:
  0.0 81.5 jit_solution(12027142989610189768)
XLA Ops:
  0.6 79.4 %strata.1 = (f32[128,256]{1,0:T(8,128)S(1)}, f32[4,128,256]{2,1,0:T(8,128)S(1)}) custom-call(f32[64,64,256]{2,1,0:T(8,128)} %bitcast.6, s32[4,6,128,128]{3,2,1,0:T(8,128)} %bitcast.7, f32[128,256]{1,0:T(8,128)} %gam_any.1, f32[1024,256]{1,0:T(8,128)} %tab_any.1, s32[4,128]{1,0:T(4,128)} %bitcast.8, s32[4,6]{1,0:T(4,128)} %bitcast.9, s32[1,4]{1,0:T(1,128)} %live_any.1), custom_call_target="tpu_custom_call" | custom-call | tf_op jit(solution)/shard_map/strata/pallas_call | solution.py:426
  80.1 0.7 copy.11
  80.7 0.8 copy.12

commit v4 on v3

--- a/solution.py
+++ b/solution.py
@@ -39,26 +39,26 @@
     v = x + 3.5
     r = 1.0 / (v * d)
     rv = r * d
-    second = (2.0 * x + 3.0) * (2.0 * q + 2.0) * (r * v)
+    second = 4.0 * ((x + 1.5) * (q + 1.0) * (r * v))
     r2 = rv * rv
     first = v + rv * (1.0 / 24.0 + r2 * (-37.0 / 5760.0 + r2 * (10313.0 / 2903040.0)))
     return first, second
 
 
-def psi_parts_wide(x):
+def minus_psi(x):
     q = x * (x + 3.0)
     v = x + 3.5
     rv = 1.0 / v
-    second = (2.0 * x + 3.0) * (2.0 / q) * ((q + 1.0) / (q + 2.0))
+    second = 4.0 * ((x + 1.5) * (q + 1.0)) * (1.0 / (q * (q + 2.0)))
     r2 = rv * rv
     first = v + rv * (1.0 / 24.0 + r2 * (-37.0 / 5760.0 + r2 * (10313.0 / 2903040.0)))
-    return first, second
+    return second - jnp.log(first)
 
 
 def kernel(
     lam_any, cnt_any, gam_any, tab_any, feat_any, cols_any, live_any,
     gout, lout,
-    lam, tab, cnt, alp, gbuf, wts, ebuf, beta, theta, ratio, part, colv, livv, featv, feat, cols, live, inv,
+    lam, tab, cnt, alp, gbuf, wts, ebuf, beta, theta, rows_log, ratio, part, colv, livv, featv, feat, cols, live, inv,
     ar_src, ar_dst, rbuf, rrecv,
     lam_sem, in_sem, id_s, id_r, ar_s, ar_r, mv_s, mv_r, rs_s, rs_r,
 ):
@@ -205,14 +205,29 @@
         for h in range(2):
             alp[t, h * HALF : (h + 1) * HALF, :] = jnp.exp(alp[t, h * HALF : (h + 1) * HALF, :])
 
+    def row_sum(value):
+        return jnp.sum(value, axis=1, keepdims=True)
+
+    def set_rows(sums, h):
+        rows_log[h * HALF : (h + 1) * HALF, :] = jnp.broadcast_to(minus_psi(sums), (HALF, TILE))
+
+    def rows_arriving(t):
+        for h in range(2):
+            set_rows(row_sum(gbuf[t, h * HALF : (h + 1) * HALF, :]), h)
+
+    def rows_staying(t):
+        for h in range(2):
+            docs = slice(h * HALF, (h + 1) * HALF)
+            set_rows(row_sum(alp[t, docs, :]) + row_sum(wts[0, docs, :] + wts[1, docs, :] + wts[2, docs, :]), h)
+
     def expect(t):
         for h in range(2):
-            g = gbuf[t, h * HALF : (h + 1) * HALF, :]
-            first, second = psi_parts(g)
-            row_first, row_second = psi_parts_wide(jnp.sum(g, axis=1, keepdims=True))
-            theta[h * HALF : (h + 1) * HALF, :] = (
-                first * (1.0 / row_first) * jnp.exp(row_second - second)
-            ).astype(jnp.bfloat16)
+            docs = slice(h * HALF, (h + 1) * HALF)
+            log_row = rows_log[docs, :]
+            for side in range(2):
+                topics = slice(side * TILE, (side + 1) * TILE)
+                first, second = psi_parts(gbuf[t, docs, topics])
+                theta[docs, topics] = (first * jnp.exp(log_row - second)).astype(jnp.bfloat16)
 
     def divide():
         th = theta[...]
@@ -267,6 +282,7 @@
             part[(s * (SLOTS + 1) + SLOTS) * 2 + h] = zero
     for copy in own_docs:
         copy.wait()
+    rows_arriving(0)
     expect(0)
     weigh(0)
     doc_prior(0)
@@ -286,6 +302,7 @@
             copy.start()
         for copy in local:
             copy.wait()
+    rows_staying(0)
     totals = sum_end(0)
 
     for t in range(STRATA):
@@ -313,19 +330,29 @@
             if t != 1:
                 alp_move(t + 1).wait_recv()
             gam_move(t).wait_recv()
+            rows_arriving(t + 1)
             expect(t + 1)
             for n in range(len(PIECES[t + 1])):
                 cnt_move(t + 1, n).wait_recv()
             weigh(t + 1)
+            rows_staying(t + 1)
             totals = 0.5 * totals + 0.5 * (WORD_PRIOR * VOCAB + GROUPS * sum_end(t + 1))
 
     give = 1 - zh
     keep = zh
     ups = (FWD_F, MRG_F, UNM_K)
+    ODD = 3
 
     def rs_copy(kind, i):
         to = across if kind == ACROSS else up if kind in ups else down
         return pltpu.make_async_remote_copy(rbuf.at[kind, i], rrecv.at[kind, i], rs_s.at[kind, i], rs_r.at[kind, i], device_id=to, device_id_type=MESH)
+
+    def odd_copy(kind, h):
+        if kind == FWD_F:
+            return pltpu.make_async_remote_copy(rbuf.at[kind, ODD], rrecv.at[kind, ODD], rs_s.at[kind, ODD], rs_r.at[kind, ODD], device_id=across, device_id_type=MESH)
+        rows_h = pl.ds(h * HALF, HALF)
+        to = up if (kind == UNM_K) != (h == 1) else down
+        return pltpu.make_async_remote_copy(rbuf.at[kind, ODD, rows_h], rrecv.at[kind, ODD, rows_h], rs_s.at[kind, ODD + h], rs_r.at[kind, ODD + h], device_id=to, device_id_type=MESH)
 
     def gathered(side, step, i, h):
         c = side * 16 + ((y + step) % NY) * 4 + i
@@ -334,23 +361,22 @@
             value = value + part[(s * (SLOTS + 1) + inv[s, c]) * 2 + h]
         return value
 
+    def fill(kind, i, side, step, h, received=()):
+        part_rows = pl.ds(h * HALF, HALF)
+        value = gathered(side, step, i, h)
+        for other in received:
+            value = value + rrecv[other, i, part_rows, :]
+        rbuf[kind, i, part_rows, :] = value
+
     def put(kind, i, side, step, received=()):
         for other in received:
             rs_copy(other, i).wait_recv()
         for h in range(2):
-            part_rows = pl.ds(h * HALF, HALF)
-            value = gathered(side, step, i, h)
-            for other in received:
-                value = value + rrecv[other, i, part_rows, :]
-            rbuf[kind, i, part_rows, :] = value
+            fill(kind, i, side, step, h, received)
         rs_copy(kind, i).start()
 
-    def each(body):
-        lax.fori_loop(0, 4, lambda i, carry: (body(i), carry)[1], 0)
-
-    def pair(first):
-        put(FWD_F, first, give, 2)
-        put(UNM_F, first, give, 3)
+    def first_three(body):
+        lax.fori_loop(0, ODD, lambda i, carry: (body(i), carry)[1], 0)
 
     def merge_give(i):
         put(MRG_F, i, give, 1, (FWD_F,))
@@ -361,32 +387,43 @@
     def send_across(i):
         put(ACROSS, i, give, 0, (UNM_F, MRG_F))
 
-    pair(0)
-    pair(1)
-    for i in (2, 3):
+    for h in range(2):
+        fill(FWD_F, ODD, give, 2, h)
+    odd_copy(FWD_F, 0).start()
+    put(MRG_F, ODD, give, 1)
+    put(UNM_F, ODD, give, 3)
+    for i in (0, 1):
+        put(FWD_F, i, give, 2)
         put(UNM_F, i, give, 3)
-    each(lambda i: put(FWD_K, i, keep, 2))
+    put(UNM_F, 2, give, 3)
+    first_three(lambda i: put(FWD_K, i, keep, 2))
+    send_across(ODD)
     merge_give(0)
     put(FWD_F, 2, give, 2)
     merge_give(1)
-    put(FWD_F, 3, give, 2)
     send_across(0)
     merge_give(2)
+    odd_copy(FWD_F, 0).wait_recv()
+    for h in range(2):
+        fill(FWD_K, ODD, keep, 2, h, (FWD_F,))
+        odd_copy(FWD_K, h).start()
+    first_three(lambda i: put(UNM_K, i, keep, 1))
+    for h in range(2):
+        fill(UNM_K, ODD, keep, 1 + 2 * h, h)
+        odd_copy(UNM_K, h).start()
+    merge_keep(0)
     send_across(1)
-    merge_keep(0)
-    merge_give(3)
-    each(lambda i: put(UNM_K, i, keep, 1))
     merge_keep(1)
+    merge_keep(2)
     send_across(2)
-    merge_keep(2)
-    send_across(3)
-    merge_keep(3)
+    for h in range(2):
+        odd_copy(FWD_K, h).wait_recv()
+        fill(MRG_K, ODD, keep, 3 - 2 * h, h, (FWD_K,))
+        odd_copy(MRG_K, h).start()
     gam_move(STRATA - 1).wait_recv()
     gout[...] = gbuf[STRATA]
 
-    def last_round(i):
-        for kind in (UNM_K, MRG_K, ACROSS):
-            rs_copy(kind, i).wait_recv()
+    def finish(i):
         for h in range(2):
             part_rows = pl.ds(h * HALF, HALF)
             value = gathered(keep, 0, i, h)
@@ -395,7 +432,17 @@
             start = lam[(grp * 4 + i) * 2 + h]
             lout[i, part_rows, :] = start * 0.0625 + (value * (1.0 / 128.0) + WORD_PRIOR * 0.9375)
 
-    each(last_round)
+    def last_round(i):
+        for kind in (UNM_K, MRG_K, ACROSS):
+            rs_copy(kind, i).wait_recv()
+        finish(i)
+
+    first_three(last_round)
+    for h in range(2):
+        odd_copy(UNM_K, h).wait_recv()
+        odd_copy(MRG_K, h).wait_recv()
+    rs_copy(ACROSS, ODD).wait_recv()
+    finish(ODD)
 
     for r in range(STRATA):
         sum_wait(r, ar_s)
@@ -414,7 +461,13 @@
         for kind in range(7):
             rs_copy(kind, i).wait_send()
 
-    each(drain)
+    first_three(drain)
+    for kind in (MRG_F, UNM_F, ACROSS):
+        rs_copy(kind, ODD).wait_send()
+    odd_copy(FWD_F, 0).wait_send()
+    for kind in (FWD_K, MRG_K, UNM_K):
+        for h in range(2):
+            odd_copy(kind, h).wait_send()
 
 
 def on_device(lambda_init, gamma_init, dmr_table, features, counts, tile_cols, live_slots):
@@ -438,6 +491,7 @@
             pltpu.VMEM((2 * SLOTS, HALF, TOPICS), f32),
             pltpu.VMEM((3, 2 * TILE, TOPICS), bf16),
             pltpu.VMEM(doc, bf16),
+            pltpu.VMEM((TILE, TILE), f32),
             pltpu.VMEM((3, TILE, 2 * TILE), bf16),
             pltpu.VMEM((STRATA * (SLOTS + 1) * 2, HALF, TOPICS), f32),
             pltpu.VMEM((STRATA, STRATA, SLOTS), i32),
@@ -459,8 +513,8 @@
             dma((STRATA,)),
             dma((16,)),
             dma((16,)),
-            dma((7, 4)),
-            dma((7, 4)),
+            dma((7, 5)),
+            dma((7, 5)),
         ],
         compiler_params=pltpu.CompilerParams(collective_id=0, has_side_effects=True),
         name="strata",

time: 81.6 us -> 78.3 us (0.960)
  Pallas kernels: 79.4 us -> 76.1 us
    pallas_call x1, Pallas kernels: 79.4 us -> 76.1 us  [on_device(): pl.pallas_call(kernel, out_shape=(pltpu.VMEM(doc, f32), pltpu.VMEM((4,) +...]
where the time goes in v4:
time: 78.3 us; the launch traced here: 78.2 us
  Pallas kernels  76.1 us (97%)
  local copies, waits for them, and re-layouts  1.45 us (2%)
    pallas_call x1, Pallas kernels, on_device(): pl.pallas_call(kernel, out_shape=(pltpu.VMEM(doc, f32), pltpu.VMEM((4,) +...  76.1 us

profile of v4, /device:TPU:1, one launch (start us, length us, event | category | flops | bytes accessed | tf_op | source)
XLA Modules:
  0.0 78.2 jit_solution(7337268282568655520)
XLA Ops:
  0.6 76.1 %strata.1 = (f32[128,256]{1,0:T(8,128)S(1)}, f32[4,128,256]{2,1,0:T(8,128)S(1)}) custom-call(f32[64,64,256]{2,1,0:T(8,128)} %bitcast.6, s32[4,6,128,128]{3,2,1,0:T(8,128)} %bitcast.7, f32[128,256]{1,0:T(8,128)} %gam_any.1, f32[1024,256]{1,0:T(8,128)} %tab_any.1, s32[4,128]{1,0:T(4,128)} %bitcast.8, s32[4,6]{1,0:T(4,128)} %bitcast.9, s32[1,4]{1,0:T(1,128)} %live_any.1), custom_call_target="tpu_custom_call" | custom-call | tf_op jit(solution)/shard_map/strata/pallas_call | solution.py:479
  76.7 0.7 copy.11
  77.4 0.8 %copy.12 = f32[512,256]{1,0:T(8,128)} copy(f32[512,256]{1,0:T(8,128)S(1)} %bitcast.5) | data formatting | bytes 1048576

commit v5 on v4

--- a/solution.py
+++ b/solution.py
@@ -124,9 +124,10 @@
     def feat_move():
         return move(feat_any, featv, 10, ORDER[2])
 
-    def gam_move(t):
+    def gam_move(t, h):
         bits = ORDER[t] ^ (ORDER[t + 1] if t + 1 < STRATA else 0)
-        return move(gbuf.at[t], gbuf.at[t + 1], 12 + t, bits)
+        rows_h = pl.ds(h * HALF, HALF)
+        return move(gbuf.at[t, rows_h], gbuf.at[t + 1, rows_h], 12 + 2 * t + h, bits)
 
     def id_moves(t):
         return [
@@ -187,7 +188,7 @@
 
     def scale_beta(totals):
         v = totals - 0.5
-        scale = 1.0 / (v + (1.0 / 24.0) / v)
+        scale = v / (v * v + 1.0 / 24.0)
         for i in range(2 * SLOTS):
             beta[i // 4, (i % 4) * HALF : (i % 4 + 1) * HALF, :] = (ebuf[i] * scale).astype(jnp.bfloat16)
 
@@ -211,17 +212,16 @@
     def set_rows(sums, h):
         rows_log[h * HALF : (h + 1) * HALF, :] = jnp.broadcast_to(minus_psi(sums), (HALF, TILE))
 
-    def rows_arriving(t):
-        for h in range(2):
-            set_rows(row_sum(gbuf[t, h * HALF : (h + 1) * HALF, :]), h)
+    def rows_arriving(t, h):
+        set_rows(row_sum(gbuf[t, h * HALF : (h + 1) * HALF, :]), h)
 
     def rows_staying(t):
         for h in range(2):
             docs = slice(h * HALF, (h + 1) * HALF)
             set_rows(row_sum(alp[t, docs, :]) + row_sum(wts[0, docs, :] + wts[1, docs, :] + wts[2, docs, :]), h)
 
-    def expect(t):
-        for h in range(2):
+    def expect(t, *halves):
+        for h in halves:
             docs = slice(h * HALF, (h + 1) * HALF)
             log_row = rows_log[docs, :]
             for side in range(2):
@@ -244,7 +244,7 @@
     def update(t):
         divide()
         gbuf[t] = alp[t] + contribution()
-        expect(t)
+        expect(t, 0, 1)
 
     def statistics(t):
         th = theta[...]
@@ -267,6 +267,9 @@
     sums = jnp.sum(acc, axis=0, keepdims=True)
     for copy in own_ids:
         copy.wait()
+    for copy in own_docs:
+        copy.wait()
+    doc_prior(0)
     pl.semaphore_wait(barrier, len(peers))
     sum_start(0, sums)
     for t in range(1, STRATA):
@@ -280,12 +283,10 @@
     for s in range(STRATA):
         for h in range(2):
             part[(s * (SLOTS + 1) + SLOTS) * 2 + h] = zero
-    for copy in own_docs:
-        copy.wait()
-    rows_arriving(0)
-    expect(0)
+    for h in range(2):
+        rows_arriving(0, h)
+        expect(0, h)
     weigh(0)
-    doc_prior(0)
     alp_move(1).start()
     feat_move().wait_recv()
     next_feat = pltpu.make_async_copy(featv, feat, in_sem.at[2])
@@ -309,7 +310,8 @@
         scale_beta(totals)
         lax.fori_loop(0, LOCAL, lambda n, carry, t=t: (update(t), carry)[1], 0)
         if t != 1:
-            gam_move(t).start()
+            for h in range(2):
+                gam_move(t, h).start()
         divide()
         if t + 1 < STRATA:
             sum_start(t + 1, jnp.sum(contribution(), axis=0, keepdims=True))
@@ -317,7 +319,8 @@
             cnt_move(2, 1).start()
             cnt_move(3, 0).start()
         if t == 1:
-            gam_move(t).start()
+            for h in range(2):
+                gam_move(t, h).start()
             cnt_move(3, 1).start()
         statistics(t)
         if t + 1 < STRATA:
@@ -329,12 +332,13 @@
                 alp_move(3).start()
             if t != 1:
                 alp_move(t + 1).wait_recv()
-            gam_move(t).wait_recv()
-            rows_arriving(t + 1)
-            expect(t + 1)
             for n in range(len(PIECES[t + 1])):
                 cnt_move(t + 1, n).wait_recv()
             weigh(t + 1)
+            for h in range(2):
+                gam_move(t, h).wait_recv()
+                rows_arriving(t + 1, h)
+                expect(t + 1, h)
             rows_staying(t + 1)
             totals = 0.5 * totals + 0.5 * (WORD_PRIOR * VOCAB + GROUPS * sum_end(t + 1))
 
@@ -420,7 +424,8 @@
         odd_copy(FWD_K, h).wait_recv()
         fill(MRG_K, ODD, keep, 3 - 2 * h, h, (FWD_K,))
         odd_copy(MRG_K, h).start()
-    gam_move(STRATA - 1).wait_recv()
+    for h in range(2):
+        gam_move(STRATA - 1, h).wait_recv()
     gout[...] = gbuf[STRATA]
 
     def finish(i):
@@ -446,7 +451,8 @@
 
     for r in range(STRATA):
         sum_wait(r, ar_s)
-        gam_move(r).wait_send()
+        for h in range(2):
+            gam_move(r, h).wait_send()
         if r > 0:
             if r == 2:
                 feat_move().wait_send()
@@ -511,8 +517,8 @@
             dma((STRATA, 2)),
             dma((STRATA,)),
             dma((STRATA,)),
-            dma((16,)),
-            dma((16,)),
+            dma((20,)),
+            dma((20,)),
             dma((7, 5)),
             dma((7, 5)),
         ],

time: 78.3 us -> 78.2 us (level)
  no operation moved by 1% of the time
where the time goes in v5:
time: 78.2 us; the launch traced here: 78.1 us
  Pallas kernels  76 us (97%)
  local copies, waits for them, and re-layouts  1.45 us (2%)
    pallas_call x1, Pallas kernels, on_device(): pl.pallas_call(kernel, out_shape=(pltpu.VMEM(doc, f32), pltpu.VMEM((4,) +...  76 us

profile of v5, /device:TPU:1, one launch (start us, length us, event | category | flops | bytes accessed | tf_op | source)
XLA Modules:
  0.0 78.1 jit_solution(8275891609199233154)
XLA Ops:
  0.6 76.0 %strata.1 = (f32[128,256]{1,0:T(8,128)S(1)}, f32[4,128,256]{2,1,0:T(8,128)S(1)}) custom-call(f32[64,64,256]{2,1,0:T(8,128)} %bitcast.6, s32[4,6,128,128]{3,2,1,0:T(8,128)} %bitcast.7, f32[128,256]{1,0:T(8,128)} %gam_any.1, f32[1024,256]{1,0:T(8,128)} %tab_any.1, s32[4,128]{1,0:T(4,128)} %bitcast.8, s32[4,6]{1,0:T(4,128)} %bitcast.9, s32[1,4]{1,0:T(1,128)} %live_any.1), custom_call_target="tpu_custom_call" | custom-call | tf_op jit(solution)/shard_map/strata/pallas_call | solution.py:485
  76.7 0.7 copy.11
  77.3 0.8 %copy.12 = f32[512,256]{1,0:T(8,128)} copy(f32[512,256]{1,0:T(8,128)S(1)} %bitcast.5) | data formatting | bytes 1048576

commit v6 on v5

--- a/solution.py
+++ b/solution.py
@@ -270,6 +270,7 @@
     for copy in own_docs:
         copy.wait()
     doc_prior(0)
+    find_slots(0)
     pl.semaphore_wait(barrier, len(peers))
     sum_start(0, sums)
     for t in range(1, STRATA):
@@ -291,7 +292,6 @@
     feat_move().wait_recv()
     next_feat = pltpu.make_async_copy(featv, feat, in_sem.at[2])
     next_feat.start()
-    find_slots(0)
     for t in range(1, STRATA):
         for copy in id_moves(t):
             copy.wait_recv()

time: 78.2 us -> 78.2 us (level)
  no operation moved by 1% of the time
where the time goes in v6:
time: 78.2 us; the launch traced here: 78.1 us
  Pallas kernels  76 us (97%)
  local copies, waits for them, and re-layouts  1.45 us (2%)
    pallas_call x1, Pallas kernels, on_device(): pl.pallas_call(kernel, out_shape=(pltpu.VMEM(doc, f32), pltpu.VMEM((4,) +...  76 us

profile of v6, /device:TPU:1, one launch (start us, length us, event | category | flops | bytes accessed | tf_op | source)
XLA Modules:
  0.0 78.1 jit_solution(9355203979392855837)
XLA Ops:
  0.6 76.0 %strata.1 = (f32[128,256]{1,0:T(8,128)S(1)}, f32[4,128,256]{2,1,0:T(8,128)S(1)}) custom-call(f32[64,64,256]{2,1,0:T(8,128)} %bitcast.6, s32[4,6,128,128]{3,2,1,0:T(8,128)} %bitcast.7, f32[128,256]{1,0:T(8,128)} %gam_any.1, f32[1024,256]{1,0:T(8,128)} %tab_any.1, s32[4,128]{1,0:T(4,128)} %bitcast.8, s32[4,6]{1,0:T(4,128)} %bitcast.9, s32[1,4]{1,0:T(1,128)} %live_any.1), custom_call_target="tpu_custom_call" | custom-call | tf_op jit(solution)/shard_map/strata/pallas_call | solution.py:485
  76.7 0.7 copy.11
  77.3 0.8 %copy.12 = f32[512,256]{1,0:T(8,128)} copy(f32[512,256]{1,0:T(8,128)S(1)} %bitcast.5) | data formatting | bytes 1048576
